TPU v7x, 256 devices: a whole 4x4x8 slice. The times are simulated.
256 devices in a mesh: seq: 64 (over z, y, core), pool: 4 (over x).
Axes of the slice: x: 4, y: 4, z: 8, core: 2. Of those that a mesh axis runs over, the one named last changes fastest.
Arguments:
- conv_input: bfloat16 [12, 4096, 10240], P('pool', 'seq'), may hold values from -6 to 6
- dt_raw: bfloat16 [12, 4096, 128], P('pool', 'seq'), may hold values from -5 to 5
- gate_z: bfloat16 [12, 4096, 8192], P('pool', 'seq'), may hold values from -6 to 6
- conv_weight: float32 [4, 10240], replicated, may hold values from -3 to 3
- dt_bias: float32 [128], P('seq'), may hold values from -2.5 to -0.5
- decay_rate: float32 [128], P('seq'), may hold values from 0.0003 to 0.05
- skip_d: float32 [128], P('seq'), may hold values from 0.5 to 1.5
- norm_gain: float32 [8192], replicated, may hold values from 0.5 to 1.5
- pool_state: bfloat16 [32, 128, 64, 128], P('pool', 'seq'), may hold values from -12 to 12
- pool_tail: bfloat16 [32, 3, 10240], P('pool'), may hold values from -6 to 6
- route_owner: int32 [12], replicated, may hold values from 0 to 3
- route_slot: int32 [12], replicated, may hold values from 0 to 7
- prefix_hit: int32 [12], replicated, may hold values 0 or 1
- lengths: int32 [12], replicated, may hold values from 1024 to 4096, as said below
Outputs:
- mixed_out: bfloat16 [12, 4096, 8192], P('pool', 'seq')
- final_state: float32 [12, 128, 64, 128], P('pool', 'seq')
Inputs may be any that keep to these rules, and one draw needn't show every extreme that they name: `lengths`: some sequence has all 4096 positions valid.
All inputs are finite; a program needn't handle non-finite values.
Results may differ from a plain program's by a relative error of at most 0.0051.
Values may be sent and summed in bfloat16 or wider, within the bound.
No kernel may reach another device: no remote copies, remote signals or barrier semaphores. Data moves between devices by JAX's collectives and lax.ppermute only.
A program may use at most 128 MiB of HBM per device.

v0:
```python
import jax
import jax.numpy as jnp
from jax import lax
from jax.sharding import PartitionSpec as P

HEADS = 128
HEAD_DIM = 64
STATE = 128
GROUPS = 8
BLOCK = 256


norm_eps = 1e-05


def conv_apply(padded_in, weight, stretch_len):
    summed = weight[0] * padded_in[..., 0:stretch_len, :]
    for offset in range(1, weight.shape[0]):
        summed = summed + weight[offset] * padded_in[..., offset : offset + stretch_len, :]
    return jax.nn.silu(summed)


def block_scan(x_part, b_part, c_part, step_size, rate, skip, start_state):
    stretch_len = x_part.shape[0]
    block_count = stretch_len // BLOCK
    lower_tri = jnp.arange(BLOCK)[:, None] >= jnp.arange(BLOCK)[None, :]

    def blocked(source):
        return source.reshape((block_count, BLOCK) + source.shape[1:])

    def per_block(carry_state, pieces):
        x_blk, b_blk, c_blk, dt_blk = pieces
        cum_decay = jnp.cumsum(-rate * dt_blk, axis=0)
        cum_heads = jnp.transpose(cum_decay, (1, 2, 0))
        log_gap = cum_heads[..., :, None] - cum_heads[..., None, :]
        decay_mat = jnp.where(lower_tri, jnp.exp(jnp.where(lower_tri, log_gap, 0.0)), 0.0)
        scores = jnp.einsum("tgn,sgn->gts", c_blk, b_blk, preferred_element_type=jnp.float32)
        dt_heads = jnp.transpose(dt_blk, (1, 2, 0))
        weights = (scores[:, None] * decay_mat * dt_heads[:, :, None, :]).astype(jnp.bfloat16)
        intra_out = jnp.einsum(
            "gets,sgep->tgep", weights, x_blk, preferred_element_type=jnp.float32
        )
        carried = jnp.exp(cum_decay)[..., None] * jnp.einsum(
            "tgn,gepn->tgep",
            c_blk.astype(jnp.float32),
            carry_state,
            precision=lax.Precision.HIGHEST,
        )
        block_out = intra_out + carried + skip[..., None] * x_blk.astype(jnp.float32)
        tail_weight = jnp.exp(cum_decay[-1][None] - cum_decay) * dt_blk
        scaled = (tail_weight[..., None] * x_blk.astype(jnp.float32)).astype(jnp.bfloat16)
        new_state = jnp.exp(cum_decay[-1])[..., None, None] * carry_state + jnp.einsum(
            "sgep,sgn->gepn", scaled, b_blk, preferred_element_type=jnp.float32
        )
        return (new_state, block_out)

    last_state, block_outs = lax.scan(
        per_block,
        start_state,
        (blocked(x_part), blocked(b_part), blocked(c_part), blocked(step_size)),
    )
    return (block_outs.reshape((stretch_len,) + block_outs.shape[2:]), last_state)


def local(
    conv_input,
    dt_raw,
    gate_z,
    conv_weight,
    dt_bias,
    decay_rate,
    skip_d,
    norm_gain,
    pool_state,
    pool_tail,
    route_owner,
    route_slot,
    prefix_hit,
    lengths,
):
    seqs_here, rows_here, channels = conv_input.shape
    seq_count = lax.axis_size("seq")
    seq_index = lax.axis_index("seq")
    pool_index = lax.axis_index("pool")
    heads_here = HEADS // seq_count
    inner_width = HEADS * HEAD_DIM
    group_heads = HEADS // GROUPS
    my_group = seq_index * heads_here // group_heads
    stretch_len = rows_here * seq_count
    slot_count = pool_state.shape[0]
    x_width = heads_here * HEAD_DIM
    x_start = seq_index * x_width
    b_start = inner_width + my_group * STATE
    c_start = inner_width + GROUPS * STATE + my_group * STATE

    def my_columns(source):
        last_dim = source.ndim - 1
        return jnp.concatenate(
            [
                lax.dynamic_slice_in_dim(source, x_start, x_width, last_dim),
                lax.dynamic_slice_in_dim(source, b_start, STATE, last_dim),
                lax.dynamic_slice_in_dim(source, c_start, STATE, last_dim),
            ],
            axis=-1,
        )

    first_seq = pool_index * seqs_here
    hit_scale = lax.dynamic_slice_in_dim(prefix_hit, first_seq, seqs_here).astype(jnp.float32)
    valid_len = lax.dynamic_slice_in_dim(lengths, first_seq, seqs_here)
    tail_source = my_columns(pool_tail)
    whole_state, whole_tail = (
        lax.all_gather(pool_state, "pool", axis=0, tiled=True),
        lax.all_gather(tail_source, "pool", axis=0, tiled=True),
    )
    own_owner = lax.dynamic_slice_in_dim(route_owner, first_seq, seqs_here)
    own_slot = lax.dynamic_slice_in_dim(route_slot, first_seq, seqs_here)
    pick_rows = own_owner * slot_count + own_slot
    seed_state = jnp.take(whole_state, pick_rows, axis=0).astype(jnp.float32)
    tail_rows = jnp.take(whole_tail, pick_rows, axis=0).astype(jnp.float32)
    seed_state = seed_state * hit_scale[:, None, None, None]
    tail_rows = tail_rows * hit_scale[:, None, None]
    local_pos = seq_index * rows_here + jnp.arange(rows_here, dtype=jnp.int32)
    mask_local = (local_pos[None, :] < valid_len[:, None]).astype(jnp.float32)
    mask_full = (jnp.arange(stretch_len, dtype=jnp.int32)[None, :] < valid_len[:, None]).astype(
        jnp.float32
    )
    x_part = conv_input[..., :inner_width].reshape(seqs_here, rows_here, seq_count, x_width)
    bc_part = conv_input[..., inner_width:].reshape(seqs_here, rows_here, 2, GROUPS, STATE)
    dt_pack = dt_raw.reshape(seqs_here, rows_here, seq_count, heads_here)
    expanded = jnp.repeat(bc_part, seq_count // GROUPS, axis=3)
    expanded = jnp.transpose(expanded, (0, 1, 3, 2, 4)).reshape(
        seqs_here, rows_here, seq_count, 2 * STATE
    )
    packed = jnp.concatenate([x_part, expanded], axis=-1)
    got_values = lax.all_to_all(packed, "seq", split_axis=2, concat_axis=1, tiled=True)
    got_dt = lax.all_to_all(dt_pack, "seq", split_axis=2, concat_axis=1, tiled=True)
    raw_heads = got_values[:, :, 0, :]
    dt_heads = got_dt[:, :, 0, :]
    padded_in = jnp.concatenate([tail_rows, raw_heads.astype(jnp.float32)], axis=1)
    conv_out = (
        conv_apply(padded_in, my_columns(conv_weight), stretch_len) * mask_full[..., None]
    ).astype(jnp.bfloat16)
    x_conv = conv_out[..., :x_width].reshape(seqs_here, stretch_len, 1, heads_here, HEAD_DIM)
    b_conv = conv_out[..., x_width : x_width + STATE].reshape(seqs_here, stretch_len, 1, STATE)
    c_conv = conv_out[..., x_width + STATE :].reshape(seqs_here, stretch_len, 1, STATE)
    step_size = jax.nn.softplus(dt_heads.astype(jnp.float32) + dt_bias) * mask_full[..., None]
    step_size = step_size.reshape(seqs_here, stretch_len, 1, heads_here)
    rate = decay_rate.reshape(1, heads_here)
    skip = skip_d.reshape(1, heads_here)
    ssd_out, last_state = jax.vmap(block_scan, in_axes=(0, 0, 0, 0, None, None, 0))(
        x_conv,
        b_conv,
        c_conv,
        step_size,
        rate,
        skip,
        seed_state.reshape(seqs_here, 1, heads_here, HEAD_DIM, STATE),
    )
    ssd_out = ssd_out.reshape(seqs_here, stretch_len, 1, x_width).astype(jnp.bfloat16)
    token_out = lax.all_to_all(ssd_out, "seq", split_axis=1, concat_axis=2, tiled=True).reshape(
        seqs_here, rows_here, inner_width
    )
    gated = token_out.astype(jnp.float32) * jax.nn.silu(gate_z.astype(jnp.float32))
    gated = gated.reshape(seqs_here, rows_here, GROUPS, inner_width // GROUPS)
    normed = gated * lax.rsqrt(jnp.mean(gated * gated, axis=-1, keepdims=True) + norm_eps)
    mixed = normed.reshape(seqs_here, rows_here, inner_width) * norm_gain * mask_local[..., None]
    final_state = last_state.reshape(seqs_here, heads_here, HEAD_DIM, STATE)
    return (mixed.astype(jnp.bfloat16), final_state)


def solution(mesh):
    in_specs = (
        P("pool", "seq", None),
        P("pool", "seq", None),
        P("pool", "seq", None),
        P(),
        P("seq"),
        P("seq"),
        P("seq"),
        P(),
        P("pool", "seq", None, None),
        P("pool", None, None),
        P(),
        P(),
        P(),
        P(),
    )
    out_specs = (P("pool", "seq", None), P("pool", "seq", None, None))
    return jax.shard_map(local, mesh=mesh, in_specs=in_specs, out_specs=out_specs, check_vma=False)
```

profile of v0, /device:TPU:1, one launch (start us, length us, event | category | flops | bytes accessed | tf_op | source)
XLA Modules:
  0.0 663.7 jit_solution(6901560358689891256)
XLA Ops:
  8.9 13.2 %all-to-all-start = ((bf16[64,2,192]{2,1,0:T(2,128)(2,1)}), bf16[64,2,192]{2,1,0:T(2,128)(2,1)S(1)}, u32[]{:S(2)}, u32[]{:S(2)}) async-start(bf16[64,2,192]{2,1,0:T(2,128)(2,1)} %reshape.473), calls=%async_computation | async-start | bytes 131072 | tf_op jit(solution)/shard_map/all_to_all | solution.py:136
  22.1 2.9 copy_bitcast_fusion.1
  25.9 5.8 broadcast_in_dim.74
  31.7 10.8 %reshape.418 = bf16[3,64,64,256]{3,1,0,2:T(8,128)(2,1)} reshape(bf16[3,64,64,2,128]{4,3,1,0,2:T(2,128)(2,1)} %bitcast.241) | data formatting | bytes 12582912 | tf_op jit(solution)/shard_map/reshape | solution.py:131
  42.5 7.9 %pad_maximum_fusion.1 = bf16[3,64,64,384]{3,1,0,2:T(8,128)(2,1)} fusion(bf16[3,64,64,256]{3,1,0,2:T(8,128)(2,1)} %reshape.418, bf16[3,64,64,128]{3,1,0,2:T(8,128)(2,1)S(1)} %copy_bitcast_fusion.1), kind=kLoop, calls=%fused_computation.65 | loop fusion | flops 18874368 | bytes 18874368 | tf_op jit(solution)/shard_map/concatenate | solution.py:134
  50.5 10.6 %all-to-all-start.1 = ((bf16[3,64,64,384]{3,1,0,2:T(8,128)(2,1)}), bf16[3,64,64,384]{3,1,0,2:T(8,128)(2,1)}, u32[]{:S(2)}, u32[]{:S(2)}) async-start(bf16[3,64,64,384]{3,1,0,2:T(8,128)(2,1)} %pad_maximum_fusion.1), calls=%async_computation.1 | async-start | bytes 18874368 | tf_op jit(solution)/shard_map/all_to_all | solution.py:135
  62.7 10.7 %all_gather.7 = bf16[32,3,384]{2,0,1:T(8,128)(2,1)S(1)} all-gather(bf16[8,3,384]{2,0,1:T(8,128)(2,1)S(1)} %pad_maximum_fusion.2), channel_id=1, replica_groups=mesh['seq'=64,'pool'=4] {'pool'}, dimensions={0}, use_global_device_ids=true | all-gather | bytes 92160 | tf_op jit(solution)/shard_map/all_gather | solution.py:113
  75.8 13.9 %all-gather.2.cloned.1.call-done = bf16[32,2,64,128]{3,2,1,0:T(8,128)(2,1)} async-done(((bf16[8,2,64,128]{3,2,1,0:T(8,128)(2,1)}), bf16[32,2,64,128]{3,2,1,0:T(8,128)(2,1)}) %all-gather.2.cloned.1.call-update) | async-done | bytes 1048592 | tf_op jit(solution)/shard_map/all_gather | solution.py:112
  89.7 1.8 gather_fusion
  91.6 174.7 %all-to-all-done.1 = bf16[3,64,64,384]{3,1,0,2:T(8,128)(2,1)} async-done(((bf16[3,64,64,384]{3,1,0,2:T(8,128)(2,1)}), bf16[3,64,64,384]{3,1,0,2:T(8,128)(2,1)}, u32[]{:S(2)}, u32[]{:S(2)}) %all-to-all-start.1) | async-done | bytes 9437216 | tf_op jit(solution)/shard_map/all_to_all | solution.py:135
  266.2 12.5 %convert_bitcast_fusion = f32[3,64,64,1,384]{4,2,0,1,3:T(8,128)} fusion(bf16[3,64,64,384]{3,1,0,2:T(8,128)(2,1)} %all-to-all-done.1), kind=kLoop, calls=%fused_computation.63 | loop fusion | flops 4718592 | bytes 28311552 | tf_op jit(solution)/shard_map/convert_element_type | solution.py:139
  278.7 7.1 %copy.164 = f32[3,64,64,1,384]{4,2,1,0,3:T(8,128)S(1)} copy(f32[3,64,64,1,384]{4,2,0,1,3:T(8,128)} %convert_bitcast_fusion) | data formatting | bytes 37748736 | tf_op jit(solution)/shard_map/convert_element_type | solution.py:139
  285.9 13.8 %multiply_convert_fusion.4 = bf16[3,4096,384]{2,1,0:T(8,128)(2,1)} fusion(f32[3,4096,384]{2,1,0:T(8,128)S(1)} %bitcast.235, f32[3,3,384]{2,1,0:T(4,128)S(1)} %convert_multiply_fusion.3, f32[3,4096]{1,0:T(4,128)S(1)} %fusion.50, f32[384]{0:T(512)S(1)} %get-tuple-element.223, f32[384]{0:T(512)S(1)} %get-tuple-element.224, f32[384]{0:T(512)S(1)} %get-tuple-element.225, ...), kind=kLoop, calls=%fused_computation.64 | loop fusion | flops 75497472 | bytes 28380672 | tf_op jit(solution)/shard_map/convert_element_type | solution.py:142
  299.6 6.8 %fusion.52 = (bf16[3,4096,128]{2,1,0:T(8,128)(2,1)}, bf16[3,4096,128]{2,1,0:T(8,128)(2,1)}, bf16[3,4096,128]{2,1,0:T(8,128)(2,1)}) fusion(bf16[3,4096,384]{2,1,0:T(8,128)(2,1)} %multiply_convert_fusion.4), kind=kLoop, calls=%fused_computation.110 | loop fusion | bytes 18874368 | tf_op jit(solution)/shard_map/slice | solution.py:145
  306.4 4.7 copy.165
  311.1 2.9 copy.188
  314.1 2.8 copy.167
  316.8 159.5 %while.16 = (s32[]{:T(128)}, f32[3,1,2,64,128]{4,3,2,0,1:T(8,128)S(1)}, bf16[16,3,256,1,2,64]{2,5,4,1,3,0:T(8,128)(2,1)}, f32[1,1,1,2]{3,2,1,0:T(1,128)S(1)}, f3...) while((s32[]{:T(128)}, ...), condition=%wide.region_3.4_spmd.clone.clone, body=%wide.region_0.3_spmd.clone.clone.sunk | while | flops 280336384 | bytes 5082009 | solution.py:57
  317.3 1.8 reduce-window.20
  322.7 2.4 fusion.76
  327.3 1.8 reduce-window.20
  331.3 1.3 fusion.75
  332.7 2.4 fusion.76
  337.2 1.8 reduce-window.20
  342.7 2.4 fusion.76
  347.2 1.8 reduce-window.20
  352.6 2.4 fusion.76
  357.2 1.8 reduce-window.20
  361.3 1.3 fusion.75
  362.6 2.4 fusion.76
  367.2 1.8 reduce-window.20
  372.6 2.4 fusion.76
  377.1 1.8 reduce-window.20
  382.5 2.4 fusion.76
  387.1 1.8 reduce-window.20
  392.5 2.4 fusion.76
  397.1 1.8 reduce-window.20
  402.5 2.4 fusion.76
  407.0 1.8 reduce-window.20
  412.5 2.4 fusion.76
  417.0 1.8 reduce-window.20
  422.4 2.4 fusion.76
  427.0 1.8 reduce-window.20
  432.4 2.4 fusion.76
  436.9 1.8 reduce-window.20
  442.4 2.4 fusion.76
  446.9 1.8 reduce-window.20
  452.3 2.4 fusion.76
  456.9 1.8 reduce-window.20
  462.3 2.4 fusion.76
  466.9 1.8 reduce-window.20
  472.3 2.4 fusion.76
  476.4 15.9 %copy.178 = bf16[3,16,256,1,2,64]{5,4,0,2,1,3:T(2,128)(2,1)} copy(bf16[3,16,256,1,2,64]{2,5,4,0,3,1:T(8,128)(2,1)} %bitcast.252) | data formatting | bytes 6291456 | tf_op jit(solution)/shard_map/convert_element_type | solution.py:159
  492.2 14.8 %reshape.468 = bf16[3,4096,1,128]{3,0,2,1:T(4,128)(2,1)} reshape(bf16[3,16,256,1,2,64]{5,4,0,2,1,3:T(2,128)(2,1)} %copy.178) | data formatting | bytes 6291456 | tf_op jit(solution)/shard_map/convert_element_type | solution.py:159
  507.0 10.7 %all-to-all-start.2 = ((bf16[3,4096,1,128]{3,0,2,1:T(4,128)(2,1)}), bf16[3,4096,1,128]{3,0,2,1:T(4,128)(2,1)}, u32[]{:S(2)}, u32[]{:S(2)}) async-start(bf16[3,4096,1,128]{3,0,2,1:T(4,128)(2,1)} %reshape.468), calls=%async_computation.2 | async-start | bytes 8388608 | tf_op jit(solution)/shard_map/all_to_all | solution.py:160
  517.8 94.3 %all-to-all-done.2 = bf16[3,4096,1,128]{3,0,2,1:T(4,128)(2,1)} async-done(((bf16[3,4096,1,128]{3,0,2,1:T(4,128)(2,1)}), bf16[3,4096,1,128]{3,0,2,1:T(4,128)(2,1)}, u32[]{:S(2)}, u32[]{:S(2)}) %all-to-all-start.2) | async-done | bytes 3145760 | tf_op jit(solution)/shard_map/all_to_all | solution.py:160
  612.1 2.6 copy.172
  615.5 6.3 copy.173
  621.8 7.3 %reshape.433 = f32[3,64,8192]{2,1,0:T(8,128)} reshape(f32[3,64,64,1,128]{4,2,1,0,3:T(8,128)} %copy.173) | data formatting | bytes 12582912 | tf_op jit(solution)/shard_map/convert_element_type | solution.py:163
  629.1 4.0 fusion.51
  633.1 6.0 copy.189
  639.7 3.1 mul.291
  642.7 7.2 %mul.292 = f32[3,64,8192]{2,1,0:T(8,128)} reshape(f32[3,64,8,1024]{3,2,1,0:T(8,128)} %mul.291) | data formatting | bytes 12582912 | tf_op jit(solution)/shard_map/mul | solution.py:165
  649.9 7.0 %multiply_convert_fusion.5 = bf16[3,64,8192]{2,1,0:T(8,128)(2,1)} fusion(f32[3,64,8192]{2,1,0:T(8,128)} %mul.292, f32[3,64]{1,0:T(4,128)S(1)} %compare_convert_fusion.1, f32[8192]{0:T(1024)S(1)} %copy-done.2, f32[3,64,8192]{2,1,0:T(8,128)} %reshape.433, bf16[3,64,8192]{2,1,0:T(8,128)(2,1)S(1)} %copy-done.1), kind=kLoop, calls=%fused_computation.74 | loop fusion | flops 15728640 | bytes 18907904 | tf_op jit(solution)/shard_map/convert_element_type | solution.py:168
  (474 shorter events, 96.0 us)
Async XLA Ops:
  8.9 41.6 %all-to-all-start = ((bf16[64,2,192]{2,1,0:T(2,128)(2,1)}), bf16[64,2,192]{2,1,0:T(2,128)(2,1)S(1)}, u32[]{:S(2)}, u32[]{:S(2)}) async-start(bf16[64,2,192]{2,1,0:T(2,128)(2,1)} %reshape.473), calls=%async_computation | async-start | bytes 131072 | tf_op jit(solution)/shard_map/all_to_all | solution.py:136
  22.1 2.9 slice-start
  50.5 23.0 %copy-start.6 = (s32[12]{0:T(128)S(1)}, s32[12]{0:T(128)}, u32[]{:S(2)}) copy-start(s32[12]{0:T(128)} %param.29) | copy-start | bytes 148
  50.5 23.1 %copy-start.4 = (s32[12]{0:T(128)S(1)}, s32[12]{0:T(128)}, u32[]{:S(2)}) copy-start(s32[12]{0:T(128)} %param.27) | copy-start | bytes 148
  50.5 23.1 %copy-start.5 = (s32[12]{0:T(128)S(1)}, s32[12]{0:T(128)}, u32[]{:S(2)}) copy-start(s32[12]{0:T(128)} %param.26) | copy-start | bytes 148
  50.5 23.7 %copy-start.7 = (s32[12]{0:T(128)S(1)}, s32[12]{0:T(128)}, u32[]{:S(2)}) copy-start(s32[12]{0:T(128)} %param.28) | copy-start | bytes 148
  50.5 24.7 %copy-start.8 = (f32[2]{0:T(128)S(1)}, f32[2]{0:T(128)}, u32[]{:S(2)}) copy-start(f32[2]{0:T(128)} %param.21) | copy-start | bytes 28
  50.5 25.2 %copy-start.3 = (f32[2]{0:T(128)S(1)}, f32[2]{0:T(128)}, u32[]{:S(2)}) copy-start(f32[2]{0:T(128)} %param.20) | copy-start | bytes 28
  50.5 215.7 %all-to-all-start.1 = ((bf16[3,64,64,384]{3,1,0,2:T(8,128)(2,1)}), bf16[3,64,64,384]{3,1,0,2:T(8,128)(2,1)}, u32[]{:S(2)}, u32[]{:S(2)}) async-start(bf16[3,64,64,384]{3,1,0,2:T(8,128)(2,1)} %pad_maximum_fusion.1), calls=%async_computation.1 | async-start | bytes 18874368 | tf_op jit(solution)/shard_map/all_to_all | solution.py:135
  61.1 28.6 %all-gather.2.cloned.1.call-start = ((), (), s32[]{:S(2)}) async-start(), calls=%async_computation.3 | async-start | bytes 1310720 | tf_op jit(solution)/shard_map/all_gather | solution.py:112
  311.1 5.7 copy-start.9
  476.3 30.7 %copy-start = (f32[3,1,2,64,128]{4,3,2,0,1:T(8,128)}, f32[3,1,2,64,128]{4,3,2,0,1:T(8,128)S(1)}, u32[]{:S(2)}) copy-start(f32[3,1,2,64,128]{4,3,2,0,1:T(8,128)S(1)} %get-tuple-element.123) | copy-start | bytes 589828
  507.0 105.1 %all-to-all-start.2 = ((bf16[3,4096,1,128]{3,0,2,1:T(4,128)(2,1)}), bf16[3,4096,1,128]{3,0,2,1:T(4,128)(2,1)}, u32[]{:S(2)}, u32[]{:S(2)}) async-start(bf16[3,4096,1,128]{3,0,2,1:T(4,128)(2,1)} %reshape.468), calls=%async_computation.2 | async-start | bytes 8388608 | tf_op jit(solution)/shard_map/all_to_all | solution.py:160
  621.8 7.3 %copy-start.1 = (bf16[3,64,8192]{2,1,0:T(8,128)(2,1)S(1)}, bf16[3,64,8192]{2,1,0:T(8,128)(2,1)}, u32[]{:S(2)}) copy-start(bf16[3,64,8192]{2,1,0:T(8,128)(2,1)} %param.18) | copy-start | bytes 9437188
  642.7 7.2 %copy-start.2 = (f32[8192]{0:T(1024)S(1)}, f32[8192]{0:T(1024)}, u32[]{:S(2)}) copy-start(f32[8192]{0:T(1024)} %param.23) | copy-start | bytes 98308
Sparse Core Ops, SparseCore 0:
  63.8 25.8 all-gather.1
where the time goes:
time: 668 us; the launch traced here: 664 us
  waiting for transfers between devices  284 us (43%)
  local copies, waits for them, and re-layouts  134 us (20%)
  matrix products  99.1 us (15%)
  other arithmetic  85.9 us (13%)
  starting transfers between devices  34.5 us (5%)
  between operations  14.4 us (2%)
  blocking collectives  10.7 us (2%)
    all_to_all x1, waiting for transfers between devices, local(): lax.all_to_all(packed, 'seq', split_axis=2, concat_axis=1, tiled=True)  175 us
    all_to_all x1, waiting for transfers between devices, local(): lax.all_to_all(ssd_out, 'seq', split_axis=1, concat_axis=2, tiled=True)  94.3 us
    dot_general x16, matrix products, per_block(): jnp.einsum('gets,sgep->tgep', weights, x_blk, preferred_element_type=jnp....  38 us
    convert_element_type x2, local copies, waits for them, and re-layouts, local(): ssd_out.reshape(seqs_here, stretch_len, 1, x_width).astype(jnp.bfloat16)  30.6 us
    another operation x48, other arithmetic  29.7 us
    dot_general x16, matrix products, per_block(): jnp.einsum('tgn,sgn->gts', c_blk, b_blk, preferred_element_type=jnp.float32)  20.5 us
    dot_general x16, matrix products, per_block(): jnp.einsum('sgep,sgn->gepn', scaled, b_blk, preferred_element_type=jnp.fl...  20.3 us
    dot_general x16, matrix products, per_block(): jnp.einsum('tgn,gepn->tgep', c_blk.astype(jnp.float32), carry_state, prec...  20.2 us
  transfers between devices with their start and end apart: 4, of which 3 were waited for; matrix products, arithmetic and copies ran while one was open for 5% of the time, Pallas kernels for 0%

commit v1 on v0

v1 whole, which is shorter than its diff:
```python
import functools

import jax
import jax.numpy as jnp
from jax import lax
from jax.experimental import pallas as pl
from jax.experimental.pallas import tpu as pltpu
from jax.sharding import Mesh, PartitionSpec as P

HEADS = 128
HEAD_DIM = 64
STATE = 128
GROUPS = 8
GROUP_HEADS = HEADS // GROUPS
INNER = HEADS * HEAD_DIM
GROUP_X = GROUP_HEADS * HEAD_DIM
GROUP_CH = GROUP_X + 2 * STATE
ROWS = 64
SLAB = GROUPS * ROWS
EXT = 16

norm_eps = 1e-05
f32 = jnp.float32
bf16 = jnp.bfloat16


def params(vmem=48):
    return pltpu.CompilerParams(vmem_limit_bytes=vmem << 20)


def silu(v):
    half = 0.5 * v
    return half + half * jnp.tanh(half)


def split3(v):
    hi = v.astype(bf16)
    rest = v - hi.astype(f32)
    mid = rest.astype(bf16)
    lo = (rest - mid.astype(f32)).astype(bf16)
    return hi, mid, lo


def lane_pack(v):
    lane = lax.broadcasted_iota(jnp.int32, v.shape, 1)
    hi, mid, lo = (part.astype(f32) for part in split3(v))
    packed = jnp.where(lane < 16, hi, jnp.where(lane < 32, mid, jnp.where(lane < 48, lo, 0.0)))
    return packed.astype(bf16)


def dot(a, b, ca=1, cb=0):
    return lax.dot_general(a, b, (((ca,), (cb,)), ((), ())), preferred_element_type=f32)


def pack_body(x_ref, b_ref, c_ref, out_ref):
    out_ref[0, :, :, 0:GROUP_X] = x_ref[...]
    out_ref[0, :, :, GROUP_X : GROUP_X + STATE] = b_ref[...]
    out_ref[0, :, :, GROUP_X + STATE : GROUP_CH] = c_ref[...]


def pack_groups(conv_input, first, count):
    block = first // count
    b_at = INNER // STATE
    return pl.pallas_call(
        pack_body,
        grid=(GROUPS,),
        in_specs=[
            pl.BlockSpec((count, ROWS, GROUP_X), lambda g: (block, 0, g)),
            pl.BlockSpec((count, ROWS, STATE), lambda g: (block, 0, b_at + g)),
            pl.BlockSpec((count, ROWS, STATE), lambda g: (block, 0, b_at + GROUPS + g)),
        ],
        out_specs=pl.BlockSpec((1, count, ROWS, GROUP_CH), lambda g: (g, 0, 0, 0)),
        out_shape=jax.ShapeDtypeStruct((GROUPS, count, ROWS, GROUP_CH), bf16),
        compiler_params=params(),
        name="pack_groups",
    )(conv_input, conv_input, conv_input)


def steps_body(meta_ref, dt_ref, par_ref, ein_ref, eout_ref, rows_ref):
    s = pl.program_id(0)
    z, j, length = meta_ref[0], meta_ref[1], meta_ref[2 + s]
    par = jnp.sum(par_ref[...], axis=0)
    bias, rate, skip = par[0:1], par[1:2], par[2:3]
    src = lax.broadcasted_iota(jnp.int32, (128, 128), 0)
    dst = lax.broadcasted_iota(jnp.int32, (128, 128), 1)
    sel = ((src == j * GROUP_HEADS + (dst & 15)) & (dst < 48)).astype(f32).astype(bf16)
    raw = dot(dt_ref[...].reshape(SLAB, 128).astype(bf16), sel)
    pos = z * SLAB + lax.broadcasted_iota(jnp.int32, (SLAB, 128), 0)
    arg = raw + bias
    dt = jnp.maximum(arg, 0.0) + jnp.log1p(jnp.exp(-jnp.abs(arg)))
    dt = jnp.where(pos < length, dt, 0.0)
    rise = -rate * dt
    row = lax.broadcasted_iota(jnp.int32, (SLAB, SLAB), 0)
    col = lax.broadcasted_iota(jnp.int32, (SLAB, SLAB), 1)
    tri = (row >= col).astype(f32).astype(bf16)
    hi, mid, lo = split3(rise)
    cum = dot(tri, hi) + dot(tri, mid) + dot(tri, lo)
    middle = 0.5 * cum[SLAB - 1 : SLAB]
    ein_ref[0] = lane_pack(jnp.exp(middle - cum) * dt)
    eout_ref[0] = lane_pack(jnp.exp(cum - middle))
    which = lax.broadcasted_iota(jnp.int32, (EXT, 128), 0)
    rows_ref[0] = lane_pack(jnp.where(which == 0, jnp.exp(middle), skip) + jnp.zeros((EXT, 128), f32))


def step_factors(meta, dt_all, par_all, seqs):
    return pl.pallas_call(
        steps_body,
        grid_spec=pltpu.PrefetchScalarGridSpec(
            num_scalar_prefetch=1,
            grid=(seqs,),
            in_specs=[
                pl.BlockSpec((GROUPS, ROWS, 128), lambda s, m: (0, s, 0)),
                pl.BlockSpec((GROUPS, 8, 128), lambda s, m: (0, 0, 0)),
            ],
            out_specs=[
                pl.BlockSpec((1, SLAB, 128), lambda s, m: (s, 0, 0)),
                pl.BlockSpec((1, SLAB, 128), lambda s, m: (s, 0, 0)),
                pl.BlockSpec((1, EXT, 128), lambda s, m: (s, 0, 0)),
            ],
        ),
        out_shape=[
            jax.ShapeDtypeStruct((seqs, SLAB, 128), bf16),
            jax.ShapeDtypeStruct((seqs, SLAB, 128), bf16),
            jax.ShapeDtypeStruct((seqs, EXT, 128), bf16),
        ],
        compiler_params=params(),
        name="step_factors",
    )(meta, dt_all, par_all)


def conv_body(first, meta_ref, recv_ref, halo_ref, w_ref, ein_ref, rows_ref, e3_ref, xbc_ref, sout_ref, xs):
    s = pl.program_id(0)
    z, length = meta_ref[0], meta_ref[2 + first + s]
    xs[0:8, :] = halo_ref[0]
    for b in range(GROUPS):
        xs[8 + ROWS * b : 8 + ROWS * (b + 1), :] = recv_ref[b, 0].astype(f32)

    def per_rows(b, _):
        start = pl.multiple_of(b * ROWS, ROWS)
        pos = z * SLAB + start + lax.broadcasted_iota(jnp.int32, (ROWS, 256), 0)
        keep = pos < length
        for lane in range(0, GROUP_CH, 256):
            win = xs[pl.ds(start, ROWS + 8), lane : lane + 256]
            acc = w_ref[3:4, lane : lane + 256] * win[8:]
            for back in (1, 2, 3):
                acc = acc + w_ref[3 - back : 4 - back, lane : lane + 256] * pltpu.roll(win, back, 0)[8:]
            xbc_ref[0, pl.ds(start, ROWS), lane : lane + 256] = jnp.where(keep, silu(acc), 0.0).astype(bf16)
        return 0

    lax.fori_loop(0, GROUPS, per_rows, 0)
    e3 = e3_ref[...]
    scaled = (xbc_ref[0, :, 0:GROUP_X].astype(f32) * dot(ein_ref[0], e3)).astype(bf16)
    state = dot(xbc_ref[0, :, GROUP_X : GROUP_X + STATE], scaled, 0, 0)
    grow = dot(rows_ref[0], e3)[0:1]
    state = (state * grow).astype(bf16)
    which = lax.broadcasted_iota(jnp.int32, (EXT, GROUP_X), 0)
    hi, mid, lo = (part.astype(f32) for part in split3(grow))
    extra = jnp.where(which == 0, hi, jnp.where(which == 1, mid, jnp.where(which == 2, lo, 0.0))).astype(bf16)
    for k in range(GROUPS):
        sout_ref[k, 0, 0:STATE, :] = state[:, 128 * k : 128 * (k + 1)]
        sout_ref[k, 0, STATE : STATE + EXT, :] = extra[:, 128 * k : 128 * (k + 1)]


def conv_and_state(meta, recv, halo, weight, ein, rows, e3, first, count):
    return pl.pallas_call(
        functools.partial(conv_body, first),
        grid_spec=pltpu.PrefetchScalarGridSpec(
            num_scalar_prefetch=1,
            grid=(count,),
            in_specs=[
                pl.BlockSpec((GROUPS, 1, ROWS, GROUP_CH), lambda s, m: (0, s, 0, 0)),
                pl.BlockSpec((1, 8, GROUP_CH), lambda s, m: (s, 0, 0)),
                pl.BlockSpec((4, GROUP_CH), lambda s, m: (0, 0)),
                pl.BlockSpec((1, SLAB, 128), lambda s, m: (first + s, 0, 0)),
                pl.BlockSpec((1, EXT, 128), lambda s, m: (first + s, 0, 0)),
                pl.BlockSpec((128, GROUP_X), lambda s, m: (0, 0)),
            ],
            out_specs=[
                pl.BlockSpec((1, SLAB, GROUP_CH), lambda s, m: (s, 0, 0)),
                pl.BlockSpec((GROUPS, 1, STATE + EXT, 128), lambda s, m: (0, s, 0, 0)),
            ],
            scratch_shapes=[pltpu.VMEM((SLAB + 8, GROUP_CH), f32)],
        ),
        out_shape=[
            jax.ShapeDtypeStruct((count, SLAB, GROUP_CH), bf16),
            jax.ShapeDtypeStruct((GROUPS, count, STATE + EXT, 128), bf16),
        ],
        compiler_params=params(),
        name="conv_and_state",
    )(meta, recv, halo, weight, ein, rows, e3)


def inner_body(xbc_ref, ein_ref, eout_ref, rows_ref, e3_ref, out_ref):
    e3 = e3_ref[...]
    x = xbc_ref[0, :, 0:GROUP_X]
    scaled = (x.astype(f32) * dot(ein_ref[0], e3)).astype(bf16)
    skip = dot(rows_ref[0], e3)[1:2]
    half = SLAB // 2
    for part in range(2):
        rows = slice(part * half, (part + 1) * half)
        upto = (part + 1) * half
        c_part = xbc_ref[0, rows, GROUP_X + STATE : GROUP_CH]
        b_part = xbc_ref[0, 0:upto, GROUP_X : GROUP_X + STATE]
        scores = dot(c_part, b_part, 1, 1)
        t_at = part * half + lax.broadcasted_iota(jnp.int32, (half, upto), 0)
        u_at = lax.broadcasted_iota(jnp.int32, (half, upto), 1)
        scores = jnp.where(u_at <= t_at, scores, 0.0).astype(bf16)
        acc = dot(scores, scaled[0:upto])
        out_ref[0, rows, :] = dot(eout_ref[0, rows, :], e3) * acc + skip * x[rows].astype(f32)


def inner_output(xbc, ein, eout, rows, e3, first, count):
    return pl.pallas_call(
        inner_body,
        grid=(count,),
        in_specs=[
            pl.BlockSpec((1, SLAB, GROUP_CH), lambda s: (s, 0, 0)),
            pl.BlockSpec((1, SLAB, 128), lambda s: (first + s, 0, 0)),
            pl.BlockSpec((1, SLAB, 128), lambda s: (first + s, 0, 0)),
            pl.BlockSpec((1, EXT, 128), lambda s: (first + s, 0, 0)),
            pl.BlockSpec((128, GROUP_X), lambda s: (0, 0)),
        ],
        out_specs=pl.BlockSpec((1, SLAB, GROUP_X), lambda s: (s, 0, 0)),
        out_shape=jax.ShapeDtypeStruct((count, SLAB, GROUP_X), f32),
        compiler_params=params(),
        name="inner_output",
    )(xbc, ein, eout, rows, e3)


def scan_body(got_ref, seed_ref, start_ref, final_ref):
    state = seed_ref[0].astype(f32).T
    for k in range(got_ref.shape[0]):
        start_ref[k, 0] = state.astype(bf16)
        extra = got_ref[k, 0, STATE : STATE + EXT, :].astype(f32)
        root = extra[0:1] + extra[1:2] + extra[2:3]
        state = (root * root) * state + got_ref[k, 0, 0:STATE, :].astype(f32)
    final_ref[0] = state.T


def scan_slabs(got, seed, first, count):
    slabs = got.shape[0]
    return pl.pallas_call(
        scan_body,
        grid=(count,),
        in_specs=[
            pl.BlockSpec((slabs, 1, STATE + EXT, 128), lambda s: (0, s, 0, 0)),
            pl.BlockSpec((1, 128, STATE), lambda s: (first + s, 0, 0)),
        ],
        out_specs=[
            pl.BlockSpec((slabs, 1, STATE, 128), lambda s: (0, s, 0, 0)),
            pl.BlockSpec((1, 128, STATE), lambda s: (s, 0, 0)),
        ],
        out_shape=[
            jax.ShapeDtypeStruct((slabs, count, STATE, 128), bf16),
            jax.ShapeDtypeStruct((count, 128, STATE), f32),
        ],
        compiler_params=params(),
        name="scan_slabs",
    )(got, seed)


def finish_body(part_ref, c_ref, start_ref, eout_ref, rows_ref, e3_ref, out_ref):
    e3 = e3_ref[...]
    grow = dot(rows_ref[0], e3)[0:1]
    state = jnp.concatenate([start_ref[k, 0] for k in range(GROUPS)], axis=1)
    carried = dot(c_ref[0], state)
    total = part_ref[0] + dot(eout_ref[0], e3) * grow * carried
    for b in range(GROUPS):
        out_ref[b, 0] = total[ROWS * b : ROWS * (b + 1)].astype(bf16)


def finish_output(part, xbc, start, eout, rows, e3, first, count):
    c_at = GROUP_CH // STATE - 1
    return pl.pallas_call(
        finish_body,
        grid=(count,),
        in_specs=[
            pl.BlockSpec((1, SLAB, GROUP_X), lambda s: (s, 0, 0)),
            pl.BlockSpec((1, SLAB, STATE), lambda s: (s, 0, c_at)),
            pl.BlockSpec((GROUPS, 1, STATE, 128), lambda s: (0, s, 0, 0)),
            pl.BlockSpec((1, SLAB, 128), lambda s: (first + s, 0, 0)),
            pl.BlockSpec((1, EXT, 128), lambda s: (first + s, 0, 0)),
            pl.BlockSpec((128, GROUP_X), lambda s: (0, 0)),
        ],
        out_specs=pl.BlockSpec((GROUPS, 1, ROWS, GROUP_X), lambda s: (0, s, 0, 0)),
        out_shape=jax.ShapeDtypeStruct((GROUPS, count, ROWS, GROUP_X), bf16),
        compiler_params=params(),
        name="finish_output",
    )(part, xbc, start, eout, rows, e3)


def norm_body(meta_ref, y_ref, gate_ref, gain_ref, out_ref):
    at = (meta_ref[0] * GROUPS + meta_ref[1]) * ROWS
    gain = gain_ref[...]
    for s in range(out_ref.shape[0]):
        gated = y_ref[0, s].astype(f32) * silu(gate_ref[s].astype(f32))
        mean = jnp.mean(gated * gated, axis=-1, keepdims=True)
        pos = at + lax.broadcasted_iota(jnp.int32, (ROWS, 1), 0)
        scale = jnp.where(pos < meta_ref[2 + s], lax.rsqrt(mean + norm_eps), 0.0)
        out_ref[s] = (gated * scale * gain).astype(bf16)


def gated_norm(meta, y, gate_z, gain, seqs):
    return pl.pallas_call(
        norm_body,
        grid_spec=pltpu.PrefetchScalarGridSpec(
            num_scalar_prefetch=1,
            grid=(GROUPS,),
            in_specs=[
                pl.BlockSpec((1, seqs, ROWS, GROUP_X), lambda g, m: (g, 0, 0, 0)),
                pl.BlockSpec((seqs, ROWS, GROUP_X), lambda g, m: (0, 0, g)),
                pl.BlockSpec((1, GROUP_X), lambda g, m: (0, g)),
            ],
            out_specs=pl.BlockSpec((seqs, ROWS, GROUP_X), lambda g, m: (0, 0, g)),
        ),
        out_shape=jax.ShapeDtypeStruct((seqs, ROWS, INNER), bf16),
        compiler_params=params(),
        name="gated_norm",
    )(meta, y, gate_z, gain)


def local(
    conv_input,
    dt_raw,
    gate_z,
    conv_weight,
    dt_bias,
    decay_rate,
    skip_d,
    norm_gain,
    pool_state,
    pool_tail,
    route_owner,
    route_slot,
    prefix_hit,
    lengths,
):
    seqs = conv_input.shape[0]
    slabs = lax.axis_size("z")
    z = lax.axis_index("z")
    j = lax.axis_index("j")
    first_seq = lax.axis_index("pool") * seqs
    slot_count = pool_state.shape[0]
    flip = [(a * GROUPS + b, b * GROUPS + a) for a in range(slabs) for b in range(GROUPS)]

    def group_columns(source):
        last = source.ndim - 1
        return jnp.concatenate(
            [
                lax.dynamic_slice_in_dim(source, j * GROUP_X, GROUP_X, last),
                lax.dynamic_slice_in_dim(source, INNER + j * STATE, STATE, last),
                lax.dynamic_slice_in_dim(source, INNER + (GROUPS + j) * STATE, STATE, last),
            ],
            axis=-1,
        )

    sent = pack_groups(conv_input, 0, seqs)
    recv = lax.all_to_all(sent, "j", 0, 0, tiled=True)

    valid_len = lax.dynamic_slice_in_dim(lengths, first_seq, seqs)
    hit = lax.dynamic_slice_in_dim(prefix_hit, first_seq, seqs)
    owner = lax.dynamic_slice_in_dim(route_owner, first_seq, seqs)
    slot = lax.dynamic_slice_in_dim(route_slot, first_seq, seqs)
    pick = owner * slot_count + slot
    meta = jnp.concatenate([jnp.stack([z, j]).astype(jnp.int32), valid_len])

    whole_state = lax.all_gather(pool_state, "pool", axis=0, tiled=True)
    seed = jnp.take(whole_state, pick, axis=0) * hit.astype(bf16)[:, None, None, None]
    seed = lax.ppermute(seed.reshape(seqs, 128, STATE), ("z", "j"), flip)

    whole_tail = lax.all_gather(group_columns(pool_tail), "pool", axis=0, tiled=True)
    tail = jnp.take(whole_tail, pick, axis=0) * hit.astype(bf16)[:, None, None]

    lane = jnp.arange(128, dtype=jnp.int32)
    own = jnp.stack([dt_bias, decay_rate, skip_d])
    here = (lane < 48) & ((lane & 15) // 2 == j)
    par = jnp.where(here, jnp.where(lane & 1 == 0, own[:, 0:1], own[:, 1:2]), 0.0)
    par = jnp.pad(par, ((0, 5), (0, 0)))
    mine = jnp.concatenate([dt_raw.reshape(seqs * ROWS, 128).astype(f32), par], axis=0)
    both = lax.all_gather(mine, "j", axis=0, tiled=False)
    par_all = lax.ppermute(both[:, seqs * ROWS :], ("z", "j"), flip)
    ein, eout, rows = step_factors(meta, both, par_all, seqs)

    head_of = jnp.arange(GROUP_X, dtype=jnp.int32)[None, :] // HEAD_DIM
    src = jnp.arange(128, dtype=jnp.int32)[:, None]
    e3 = ((src < 48) & ((src & 15) == head_of)).astype(bf16)
    weight = group_columns(conv_weight)

    before = lax.ppermute(recv[GROUPS - 1, :, ROWS - 3 :], "z", [(k, k + 1) for k in range(slabs - 1)])
    halo = jnp.where(z == 0, tail, before).astype(f32)
    halo = jnp.pad(halo, ((0, 0), (5, 0), (0, 0)))

    xbc, sout = conv_and_state(meta, recv, halo, weight, ein, rows, e3, 0, seqs)
    got = lax.all_to_all(sout, "z", 0, 0, tiled=True)
    part = inner_output(xbc, ein, eout, rows, e3, 0, seqs)
    start, final = scan_slabs(got, seed, 0, seqs)
    back = lax.all_to_all(start, "z", 0, 0, tiled=True)
    final = lax.ppermute(final, ("z", "j"), flip)
    y = finish_output(part, xbc, back, eout, rows, e3, 0, seqs)
    token = lax.all_to_all(y, "j", 0, 0, tiled=True)
    mixed = gated_norm(meta, token, gate_z, norm_gain.reshape(1, INNER), seqs)
    return (mixed, final.reshape(seqs, 2, HEAD_DIM, STATE))


def solution(mesh):
    seq_count, pool_count = mesh.devices.shape
    split = Mesh(mesh.devices.reshape(seq_count // GROUPS, GROUPS, pool_count), ("z", "j", "pool"))
    seq = ("z", "j")
    in_specs = (
        P("pool", seq, None),
        P("pool", seq, None),
        P("pool", seq, None),
        P(),
        P(seq),
        P(seq),
        P(seq),
        P(),
        P("pool", seq, None, None),
        P("pool", None, None),
        P(),
        P(),
        P(),
        P(),
    )
    out_specs = (P("pool", seq, None), P("pool", seq, None, None))
    return jax.shard_map(local, mesh=split, in_specs=in_specs, out_specs=out_specs, check_vma=False)
```

time: 668 us -> 250 us (0.37)
  waiting for transfers between devices: 284 us -> 68.5 us
  local copies, waits for them, and re-layouts: 134 us -> 15.6 us
  matrix products: 99.1 us -> 0 us
  other arithmetic: 85.9 us -> 0.74 us
  blocking collectives: 10.7 us -> 64.6 us
  Pallas kernels: 0 us -> 39.3 us
  starting transfers between devices: 34.5 us -> 46.1 us
    all_to_all x3 -> x4, waiting for transfers between devices: 269 us -> 51.9 us  [the longest x1 34.8 us: local(): token = lax.all_to_all(y, 'j', 0, 0, tiled=True)]
    dot_general x64 -> x0, matrix products: 99.1 us -> none  [the longest x16 38 us: per_block(): jnp.einsum('gets,sgep->tgep', weights, x_blk, preferred_element_type=jnp....]
    all_gather x1 -> x2, blocking collectives: 10.7 us -> 64.6 us  [the longest x1 54.1 us: local(): both = lax.all_gather(mine, 'j', axis=0, tiled=False)]
    convert_element_type x7 -> x0, local copies, waits for them, and re-layouts: 51.5 us -> none  [the longest x2 30.6 us: local(): ssd_out.reshape(seqs_here, stretch_len, 1, x_width).astype(jnp.bfloat16)]
    pallas_call x0 -> x7, Pallas kernels: none -> 39.3 us  [the longest x1 10.2 us: conv_and_state(): pl.pallas_call(functools.partial(conv_body, first), grid_spec=pltpu.Prefe...]
    convert_element_type x9 -> x3, other arithmetic: 34.3 us -> 0.25 us  [the longest x1 0.15 us: local(): e3 = ((src < 48) & (src & 15 == head_of)).astype(bf16)]
    another operation x48 -> x1, other arithmetic: 29.7 us -> 0.01 us  [local(): own = jnp.stack([dt_bias, decay_rate, skip_d])]
    ppermute x0 -> x4, waiting for transfers between devices: none -> 15.8 us  [the longest x1 10.6 us: local(): seed = lax.ppermute(seed.reshape(seqs, 128, STATE), ('z', 'j'), flip)]
  transfers between devices with their start and end apart: 4 -> 9, of which waited for: 3 -> 5; matrix products, arithmetic and copies ran while one was open for 5% -> 3% of each run, Pallas kernels for 0% -> 8%
where the time goes in v1:
time: 250 us; the launch traced here: 249 us
  waiting for transfers between devices  68.5 us (27%)
  blocking collectives  64.6 us (26%)
  starting transfers between devices  46.1 us (18%)
  Pallas kernels  39.3 us (16%)
  local copies, waits for them, and re-layouts  15.6 us (6%)
  between operations  14.3 us (6%)
    all_gather x1, blocking collectives, local(): both = lax.all_gather(mine, 'j', axis=0, tiled=False)  54.1 us
    all_to_all x1, waiting for transfers between devices, local(): token = lax.all_to_all(y, 'j', 0, 0, tiled=True)  34.8 us
    all_to_all x1, waiting for transfers between devices, local(): back = lax.all_to_all(start, 'z', 0, 0, tiled=True)  14.3 us
    all_to_all x1, starting transfers between devices, local(): back = lax.all_to_all(start, 'z', 0, 0, tiled=True)  11.3 us
    ppermute x1, waiting for transfers between devices, local(): seed = lax.ppermute(seed.reshape(seqs, 128, STATE), ('z', 'j'), flip)  10.6 us
    all_gather x1, blocking collectives, local(): lax.all_gather(group_columns(pool_tail), 'pool', axis=0, tiled=True)  10.5 us
    pallas_call x1, Pallas kernels, conv_and_state(): pl.pallas_call(functools.partial(conv_body, first), grid_spec=pltpu.Prefe...  10.2 us
    unnamed x31, local copies, waits for them, and re-layouts  9 us
  transfers between devices with their start and end apart: 9, of which 5 were waited for; matrix products, arithmetic and copies ran while one was open for 3% of the time, Pallas kernels for 8%

profile of v1, /device:TPU:1, one launch (start us, length us, event | category | flops | bytes accessed | tf_op | source)
XLA Modules:
  0.0 249.1 jit_solution(570805154283601393)
XLA Ops:
  7.2 4.7 %pack_groups.1 = bf16[8,3,64,1280]{3,2,1,0:T(8,128)(2,1)S(1)} custom-call(bf16[3,64,10240]{2,1,0:T(8,128)(2,1)} %c_ref.1, bf16[3,64,10240]{2,1,0:T(8,128)(2,1)} %c_ref.1, bf16[3,64,10240]{2,1,0:T(8,128)(2,1)} %c_ref.1), custom_call_target="tpu_custom_call" | custom-call | tf_op jit(solution)/shard_map/pack_groups/pallas_call | solution.py:64
  11.8 0.0 copy-start
  11.8 1.9 copy-done
  13.7 0.0 copy-start.13
  13.7 0.0 copy-start.14
  13.7 0.0 copy-start.11
  13.8 0.0 copy-start.12
  13.8 7.8 %all-to-all-start = ((bf16[8,3,64,1280]{3,2,1,0:T(8,128)(2,1)}), bf16[8,3,64,1280]{3,2,1,0:T(8,128)(2,1)}, u32[]{:S(2)}, u32[]{:S(2)}) async-start(bf16[8,3,64,1280]{3,2,1,0:T(8,128)(2,1)} %copy-done), calls=%async_computation | async-start | bytes 7864320 | tf_op jit(solution)/shard_map/all_to_all | solution.py:358
  21.6 0.0 all-gather.3.cloned.1.call-start
  21.6 0.7 all-gather.3.cloned.1.call-update
  22.3 0.0 copy-done.8
  22.3 0.0 copy-done.9
  22.3 0.0 copy-done.10
  22.4 0.2 slice_reduce_fusion.1
  22.5 0.1 select_select_fusion
  22.6 0.0 copy-done.7
  22.7 54.1 %all-gather = f32[1600,128]{1,0:T(8,128)S(1)} all-gather(f32[200,128]{1,0:T(8,128)S(1)} %select_maximum_fusion), channel_id=2, replica_groups=mesh['z'=8,'j'=8,'pool'=4] {'j'}, dimensions={0}, use_global_device_ids=true | all-gather | bytes 921600 | tf_op jit(solution)/shard_map/all_gather | solution.py:380
  76.8 1.9 collective-permute-start.1
  78.7 0.0 copy-done.13
  78.7 0.1 dynamic_slice.30
  78.8 0.0 copy-done.14
  78.8 0.1 dynamic-slice_convert_fusion
  78.9 0.1 pad_add_fusion.meta_ref
  78.9 0.0 copy-done.12
  78.9 0.1 compare_and_fusion.1
  79.0 0.7 constant_dynamic-slice_fusion.1
  79.7 0.7 constant_dynamic-slice_fusion.4
  80.5 0.7 constant_dynamic-slice_fusion.2
  81.2 0.8 constant_dynamic-slice_fusion.5
  82.0 0.1 and_convert_fusion.e3_ref
  82.2 0.0 all-to-all-done.recv_ref
  82.2 0.8 slice_bitcast_fusion
  83.0 1.3 collective-permute-start
  84.3 10.5 %all_gather.12 = bf16[32,3,1280]{2,0,1:T(8,128)(2,1)S(1)} all-gather(bf16[8,3,1280]{2,0,1:T(8,128)(2,1)S(1)} %pad_maximum_fusion), channel_id=1, replica_groups=mesh['z'=8,'j'=8,'pool'=4] {'pool'}, dimensions={0}, use_global_device_ids=true | all-gather | bytes 307200 | tf_op jit(solution)/shard_map/all_gather | solution.py:371
  94.8 0.2 copy.19
  95.0 0.6 gather_fusion
  95.6 0.0 collective-permute-done.1.par_ref
  95.6 4.2 %step_factors.1 = (bf16[3,512,128]{2,1,0:T(8,128)(2,1)S(1)}, bf16[3,512,128]{2,1,0:T(8,128)(2,1)S(1)}, bf16[3,16,128]{2,1,0:T(8,128)(2,1)S(1)}) custom-call(s32[5]{0:T(128)S(1)} %pad_add_fusion.meta_ref, f32[8,200,128]{2,1,0:T(8,128)S(1)} %bitcast.18, f32[8,8,128]{2,1,0:T(8,128)S(1)} %collective-permute-done.1.par_ref), custom_call_target="tpu_custom_call" | custom-call | tf_op jit(solution)/shard_map/step_factors/pallas_call | solution.py:106
  99.9 0.0 collective-permute-done
  99.9 0.1 multiply_select_fusion
  100.0 10.2 %conv_and_state.1 = (bf16[3,512,1280]{2,1,0:T(8,128)(2,1)S(1)}, bf16[8,3,144,128]{3,2,1,0:T(8,128)(2,1)}) custom-call(s32[5]{0:T(128)S(1)} %pad_add_fusion.meta_ref, bf16[8,3,64,1280]{3,2,1,0:T(8,128)(2,1)} %all-to-all-done.recv_ref, f32[3,8,1280]{2,1,0:T(8,128)S(1)} %pad_convert_fusion.halo_ref, f32[4,1280]{1,0:T(4,128)S(1)} %pad_maximum_fusion.1.w_ref, ...), custom_call_target="tpu_custom_call" | custom-call | tf_op jit(solution)/shard_map/conv_and_state/pallas_call | solution.py:165
  110.2 1.9 copy-done.1
  112.2 7.6 %all-to-all-start.1 = ((bf16[8,3,144,128]{3,2,1,0:T(8,128)(2,1)}), bf16[8,3,144,128]{3,2,1,0:T(8,128)(2,1)S(1)}, u32[]{:S(2)}, u32[]{:S(2)}) async-start(bf16[8,3,144,128]{3,2,1,0:T(8,128)(2,1)} %get-tuple-element.13), calls=%async_computation.1 | async-start | bytes 1769472 | tf_op jit(solution)/shard_map/all_to_all | solution.py:394
  119.7 0.0 all-gather.3.cloned.1.call-done
  119.7 1.8 gather_fusion.1
  121.5 0.1 fusion
  121.6 7.1 %collective-permute-start.2 = (bf16[3,128,128]{2,1,0:T(8,128)(2,1)S(1)}, bf16[3,128,128]{2,1,0:T(8,128)(2,1)S(1)}, u32[]{:S(2)}, u32[]{:S(2)}) collective-permute-start(bf16[3,128,128]{2,1,0:T(8,128)(2,1)S(1)} %fusion), channel_id=1, source_target_pairs={{0,0},{4,32},{8,64},{12,96},{16,128},{20,160},{24,192},{28,224},{3... | collective-permute-start | bytes 294920 | tf_op jit(solution)/shard_map/ppermute | solution.py:369
  128.8 10.6 %collective-permute-done.2.seed_ref = bf16[3,128,128]{2,1,0:T(8,128)(2,1)S(1)} collective-permute-done((bf16[3,128,128]{2,1,0:T(8,128)(2,1)S(1)}, bf16[3,128,128]{2,1,0:T(8,128)(2,1)S(1)}, u32[]{:S(2)}, u32[]{:S(2)}) %collective-permute-start.2) | collective-permute-done | bytes 98336 | tf_op jit(solution)/shard_map/ppermute | solution.py:369
  139.4 2.8 %all-to-all-done.1.got_ref = bf16[8,3,144,128]{3,2,1,0:T(8,128)(2,1)S(1)} async-done(((bf16[8,3,144,128]{3,2,1,0:T(8,128)(2,1)}), bf16[8,3,144,128]{3,2,1,0:T(8,128)(2,1)S(1)}, u32[]{:S(2)}, u32[]{:S(2)}) %all-to-all-start.1) | async-done | bytes 884768 | tf_op jit(solution)/shard_map/all_to_all | solution.py:394
  142.2 1.9 scan_slabs.1
  144.1 11.3 %all-to-all-start.2 = ((bf16[8,3,128,128]{3,2,1,0:T(8,128)(2,1)}), bf16[8,3,128,128]{3,2,1,0:T(8,128)(2,1)S(1)}, u32[]{:S(2)}, u32[]{:S(2)}) async-start(bf16[8,3,128,128]{3,2,1,0:T(8,128)(2,1)} %get-tuple-element.14), calls=%async_computation.2 | async-start | bytes 1572864 | tf_op jit(solution)/shard_map/all_to_all | solution.py:397
  155.4 2.1 copy-done.2
  157.5 5.7 %inner_output.1.part_ref = f32[3,512,1024]{2,1,0:T(8,128)} custom-call(bf16[3,512,1280]{2,1,0:T(8,128)(2,1)S(1)} %copy-done.2, bf16[3,512,128]{2,1,0:T(8,128)(2,1)S(1)} %get-tuple-element.9.ein_ref, bf16[3,512,128]{2,1,0:T(8,128)(2,1)S(1)} %get-tuple-element.12.eout_ref, bf16[3,16,128]{2,1,0:T(8,128)(2,1)S(1)} %get-tuple-element.10.rows_ref, ...), custom_call_target="tpu_custom_call" | custom-call | tf_op jit(solution)/shard_map/inner_output/pallas_call | solution.py:213
  163.2 14.3 %all-to-all-done.2.start_ref = bf16[8,3,128,128]{3,2,1,0:T(8,128)(2,1)S(1)} async-done(((bf16[8,3,128,128]{3,2,1,0:T(8,128)(2,1)}), bf16[8,3,128,128]{3,2,1,0:T(8,128)(2,1)S(1)}, u32[]{:S(2)}, u32[]{:S(2)}) %all-to-all-start.2) | async-done | bytes 786464 | tf_op jit(solution)/shard_map/all_to_all | solution.py:397
  177.5 4.8 %finish_output.1 = bf16[8,3,64,1024]{3,2,1,0:T(8,128)(2,1)S(1)} custom-call(f32[3,512,1024]{2,1,0:T(8,128)} %inner_output.1.part_ref, bf16[3,512,1280]{2,1,0:T(8,128)(2,1)} %copy-done.1, bf16[8,3,128,128]{3,2,1,0:T(8,128)(2,1)S(1)} %all-to-all-done.2.start_ref, bf16[3,512,128]{2,1,0:T(8,128)(2,1)S(1)} %get-tuple-element.12.eout_ref, ...), custom_call_target="tpu_custom_call" | custom-call | tf_op jit(solution)/shard_map/finish_output/pallas_call | solution.py:274
  182.4 0.0 copy-start.3
  182.4 1.7 copy-done.3
  184.1 6.9 %all-to-all-start.3 = ((bf16[8,3,64,1024]{3,2,1,0:T(8,128)(2,1)}), bf16[8,3,64,1024]{3,2,1,0:T(8,128)(2,1)S(1)}, u32[]{:S(2)}, u32[]{:S(2)}) async-start(bf16[8,3,64,1024]{3,2,1,0:T(8,128)(2,1)} %copy-done.3), calls=%async_computation.3 | async-start | bytes 6291456 | tf_op jit(solution)/shard_map/all_to_all | solution.py:400
  191.0 2.1 collective-permute-start.3
  193.1 5.2 %collective-permute-done.3 = f32[3,128,128]{2,1,0:T(8,128)S(1)} collective-permute-done((f32[3,128,128]{2,1,0:T(8,128)S(1)}, f32[3,128,128]{2,1,0:T(8,128)S(1)}, u32[]{:S(2)}, u32[]{:S(2)}) %collective-permute-start.3) | collective-permute-done | bytes 196640 | tf_op jit(solution)/shard_map/ppermute | solution.py:398
  198.3 0.7 copy-done.5
  198.9 34.8 %all-to-all-done.3.y_ref = bf16[8,3,64,1024]{3,2,1,0:T(8,128)(2,1)S(1)} async-done(((bf16[8,3,64,1024]{3,2,1,0:T(8,128)(2,1)}), bf16[8,3,64,1024]{3,2,1,0:T(8,128)(2,1)S(1)}, u32[]{:S(2)}, u32[]{:S(2)}) %all-to-all-start.3) | async-done | bytes 3145760 | tf_op jit(solution)/shard_map/all_to_all | solution.py:400
  233.8 7.8 %gated_norm.1 = bf16[3,64,8192]{2,1,0:T(8,128)(2,1)} custom-call(s32[5]{0:T(128)S(1)} %pad_add_fusion.meta_ref, bf16[8,3,64,1024]{3,2,1,0:T(8,128)(2,1)S(1)} %all-to-all-done.3.y_ref, bf16[3,64,8192]{2,1,0:T(8,128)(2,1)} %gate_ref.1, f32[1,8192]{1,0:T(1,128)S(1)} %bitcast.19), custom_call_target="tpu_custom_call" | custom-call | tf_op jit(solution)/shard_map/gated_norm/pallas_call | solution.py:304
  241.6 0.7 copy.21
  (24 shorter events, 0.1 us)
Async XLA Ops:
  11.8 1.9 copy-start
  13.7 8.6 %copy-start.8 = (f32[2]{0:T(128)S(1)}, f32[2]{0:T(128)}, u32[]{:S(2)}) copy-start(f32[2]{0:T(128)} %param.20) | copy-start | bytes 28
  13.7 8.6 %copy-start.9 = (f32[2]{0:T(128)S(1)}, f32[2]{0:T(128)}, u32[]{:S(2)}) copy-start(f32[2]{0:T(128)} %param.19) | copy-start | bytes 28
  13.7 8.6 %copy-start.10 = (f32[2]{0:T(128)S(1)}, f32[2]{0:T(128)}, u32[]{:S(2)}) copy-start(f32[2]{0:T(128)} %param.18) | copy-start | bytes 28
  13.7 8.9 %copy-start.7 = (bf16[3,64,128]{2,1,0:T(8,128)(2,1)S(1)}, bf16[3,64,128]{2,1,0:T(8,128)(2,1)}, u32[]{:S(2)}) copy-start(bf16[3,64,128]{2,1,0:T(8,128)(2,1)} %param.15) | copy-start | bytes 147460
  13.7 65.0 %copy-start.13 = (s32[12]{0:T(128)S(1)}, s32[12]{0:T(128)}, u32[]{:S(2)}) copy-start(s32[12]{0:T(128)} %param.27) | copy-start | bytes 148
  13.7 65.0 %copy-start.14 = (s32[12]{0:T(128)S(1)}, s32[12]{0:T(128)}, u32[]{:S(2)}) copy-start(s32[12]{0:T(128)} %param.26) | copy-start | bytes 148
  13.7 65.2 %copy-start.11 = (s32[12]{0:T(128)S(1)}, s32[12]{0:T(128)}, u32[]{:S(2)}) copy-start(s32[12]{0:T(128)} %param.25) | copy-start | bytes 148
  13.8 65.2 %copy-start.12 = (s32[12]{0:T(128)S(1)}, s32[12]{0:T(128)}, u32[]{:S(2)}) copy-start(s32[12]{0:T(128)} %param.24) | copy-start | bytes 148
  13.8 68.4 %all-to-all-start = ((bf16[8,3,64,1280]{3,2,1,0:T(8,128)(2,1)}), bf16[8,3,64,1280]{3,2,1,0:T(8,128)(2,1)}, u32[]{:S(2)}, u32[]{:S(2)}) async-start(bf16[8,3,64,1280]{3,2,1,0:T(8,128)(2,1)} %copy-done), calls=%async_computation | async-start | bytes 7864320 | tf_op jit(solution)/shard_map/all_to_all | solution.py:358
  21.6 98.1 %all-gather.3.cloned.1.call-start = ((), (), s32[]{:S(2)}) async-start(), calls=%async_computation.4 | async-start | bytes 1310720 | tf_op jit(solution)/shard_map/all_gather | solution.py:367
  76.8 18.9 %collective-permute-start.1 = (f32[8,8,128]{2,1,0:T(8,128)S(1)}, f32[8,8,128]{2,1,0:T(8,128)S(1)}, u32[]{:S(2)}, u32[]{:S(2)}) collective-permute-start(f32[8,8,128]{2,1,0:T(8,128)S(1)} %slice.21), channel_id=1, source_target_pairs={{0,0},{4,32},{8,64},{12,96},{16,128},{20,160},{24,192},{28,224},{3... | collective-permute-start | bytes 98312 | tf_op jit(solution)/shard_map/ppermute | solution.py:381
  83.0 16.8 %collective-permute-start = (bf16[3,3,1280]{2,1,0:T(4,128)(2,1)S(1)}, bf16[3,3,1280]{2,1,0:T(4,128)(2,1)S(1)}, u32[]{:S(2)}, u32[]{:S(2)}) collective-permute-start(bf16[3,3,1280]{2,1,0:T(4,128)(2,1)S(1)} %slice_bitcast_fusion), channel_id=1, source_target_pairs={{0,32},{32,64},{64,96},{96,128},{128,160},{160,192},{192,224},{1,3... | collective-permute-start | bytes 69128 | tf_op jit(solution)/shard_map/ppermute | solution.py:389
  110.2 1.9 copy-start.1
  112.2 30.0 %all-to-all-start.1 = ((bf16[8,3,144,128]{3,2,1,0:T(8,128)(2,1)}), bf16[8,3,144,128]{3,2,1,0:T(8,128)(2,1)S(1)}, u32[]{:S(2)}, u32[]{:S(2)}) async-start(bf16[8,3,144,128]{3,2,1,0:T(8,128)(2,1)} %get-tuple-element.13), calls=%async_computation.1 | async-start | bytes 1769472 | tf_op jit(solution)/shard_map/all_to_all | solution.py:394
  121.6 17.8 %collective-permute-start.2 = (bf16[3,128,128]{2,1,0:T(8,128)(2,1)S(1)}, bf16[3,128,128]{2,1,0:T(8,128)(2,1)S(1)}, u32[]{:S(2)}, u32[]{:S(2)}) collective-permute-start(bf16[3,128,128]{2,1,0:T(8,128)(2,1)S(1)} %fusion), channel_id=1, source_target_pairs={{0,0},{4,32},{8,64},{12,96},{16,128},{20,160},{24,192},{28,224},{3... | collective-permute-start | bytes 294920 | tf_op jit(solution)/shard_map/ppermute | solution.py:369
  144.1 33.5 %all-to-all-start.2 = ((bf16[8,3,128,128]{3,2,1,0:T(8,128)(2,1)}), bf16[8,3,128,128]{3,2,1,0:T(8,128)(2,1)S(1)}, u32[]{:S(2)}, u32[]{:S(2)}) async-start(bf16[8,3,128,128]{3,2,1,0:T(8,128)(2,1)} %get-tuple-element.14), calls=%async_computation.2 | async-start | bytes 1572864 | tf_op jit(solution)/shard_map/all_to_all | solution.py:397
  155.4 2.1 copy-start.2
  182.4 1.7 copy-start.3
  184.0 49.7 %copy-start.4 = (f32[8192]{0:T(1024)S(1)}, f32[8192]{0:T(1024)}, u32[]{:S(2)}) copy-start(f32[8192]{0:T(1024)} %param.21) | copy-start | bytes 98308
  184.1 49.7 %all-to-all-start.3 = ((bf16[8,3,64,1024]{3,2,1,0:T(8,128)(2,1)}), bf16[8,3,64,1024]{3,2,1,0:T(8,128)(2,1)S(1)}, u32[]{:S(2)}, u32[]{:S(2)}) async-start(bf16[8,3,64,1024]{3,2,1,0:T(8,128)(2,1)} %copy-done.3), calls=%async_computation.3 | async-start | bytes 6291456 | tf_op jit(solution)/shard_map/all_to_all | solution.py:400
  191.0 7.3 %collective-permute-start.3 = (f32[3,128,128]{2,1,0:T(8,128)S(1)}, f32[3,128,128]{2,1,0:T(8,128)S(1)}, u32[]{:S(2)}, u32[]{:S(2)}) collective-permute-start(f32[3,128,128]{2,1,0:T(8,128)S(1)} %get-tuple-element.15), channel_id=1, source_target_pairs={{0,0},{4,32},{8,64},{12,96},{16,128},{20,160},{24,192},{28,224},{3... | collective-permute-start | bytes 589832 | tf_op jit(solution)/shard_map/ppermute | solution.py:398
  198.3 0.7 copy-start.5
  233.8 7.8 %copy-start.6 = (f32[3,128,128]{2,1,0:T(8,128)S(1)}, f32[3,128,128]{2,1,0:T(8,128)}, u32[]{:S(2)}) copy-start(f32[3,128,128]{2,1,0:T(8,128)} %copy-done.5) | copy-start | bytes 589828
Sparse Core Ops, SparseCore 0:
  24.2 26.5 all-gather.2

commit v2 on v1

--- a/solution.py
+++ b/solution.py
@@ -24,7 +24,7 @@
 bf16 = jnp.bfloat16
 
 
-def params(vmem=48):
+def params(vmem=24):
     return pltpu.CompilerParams(vmem_limit_bytes=vmem << 20)
 
 
@@ -52,39 +52,90 @@
     return lax.dot_general(a, b, (((ca,), (cb,)), ((), ())), preferred_element_type=f32)
 
 
-def pack_body(x_ref, b_ref, c_ref, out_ref):
-    out_ref[0, :, :, 0:GROUP_X] = x_ref[...]
-    out_ref[0, :, :, GROUP_X : GROUP_X + STATE] = b_ref[...]
-    out_ref[0, :, :, GROUP_X + STATE : GROUP_CH] = c_ref[...]
+def in_hbm(v):
+    return pltpu.with_memory_space_constraint(v, pltpu.HBM)
+
+
+def pack_body(first, x_ref, out_ref, held, in_sems, out_sems):
+    count = held.shape[0]
+    loads = [pltpu.make_async_copy(x_ref.at[first + s], held.at[s], in_sems.at[s]) for s in range(count)]
+    for load in loads:
+        load.start()
+    stores = []
+    for s in range(count):
+        loads[s].wait()
+        for g in range(GROUPS):
+            pieces = (
+                (g * GROUP_X, 0, GROUP_X),
+                (INNER + g * STATE, GROUP_X, STATE),
+                (INNER + (GROUPS + g) * STATE, GROUP_X + STATE, STATE),
+            )
+            for i, (src, dst, width) in enumerate(pieces):
+                store = pltpu.make_async_copy(
+                    held.at[s, :, pl.ds(src, width)],
+                    out_ref.at[g, s, :, pl.ds(dst, width)],
+                    out_sems.at[s, g, i],
+                )
+                store.start()
+                stores.append(store)
+    for store in stores:
+        store.wait()
 
 
 def pack_groups(conv_input, first, count):
-    block = first // count
-    b_at = INNER // STATE
-    return pl.pallas_call(
-        pack_body,
-        grid=(GROUPS,),
-        in_specs=[
-            pl.BlockSpec((count, ROWS, GROUP_X), lambda g: (block, 0, g)),
-            pl.BlockSpec((count, ROWS, STATE), lambda g: (block, 0, b_at + g)),
-            pl.BlockSpec((count, ROWS, STATE), lambda g: (block, 0, b_at + GROUPS + g)),
-        ],
-        out_specs=pl.BlockSpec((1, count, ROWS, GROUP_CH), lambda g: (g, 0, 0, 0)),
-        out_shape=jax.ShapeDtypeStruct((GROUPS, count, ROWS, GROUP_CH), bf16),
-        compiler_params=params(),
+    return pl.pallas_call(
+        functools.partial(pack_body, first),
+        in_specs=[pl.BlockSpec(memory_space=pl.ANY)],
+        out_specs=pl.BlockSpec(memory_space=pl.ANY),
+        out_shape=pltpu.HBM((GROUPS, count, ROWS, GROUP_CH), bf16),
+        scratch_shapes=[
+            pltpu.VMEM((count,) + conv_input.shape[1:], bf16),
+            pltpu.SemaphoreType.DMA((count,)),
+            pltpu.SemaphoreType.DMA((count, GROUPS, 3)),
+        ],
+        compiler_params=params(12),
         name="pack_groups",
-    )(conv_input, conv_input, conv_input)
+    )(in_hbm(conv_input))
+
+
+def front_body(j_ref, bias_ref, rate_ref, skip_ref, dt_ref, out_ref):
+    row = lax.broadcasted_iota(jnp.int32, (EXT, 128), 0)
+    lane = lax.broadcasted_iota(jnp.int32, (EXT, 128), 1)
+    even = (lane & 1) == 0
+    values = jnp.where(even, skip_ref[0], skip_ref[1])
+    values = jnp.where(row == 0, jnp.where(even, bias_ref[0], bias_ref[1]), values)
+    values = jnp.where(row == 1, jnp.where(even, rate_ref[0], rate_ref[1]), values)
+    here = ((lane & 15) >> 1 == j_ref[0]) & (row < 3)
+    packed = lane_pack(jnp.where(here, values, 0.0))
+    rows = dt_ref.shape[0]
+    for g in range(GROUPS):
+        out_ref[g, 0:rows, :] = dt_ref[...]
+        out_ref[g, rows : rows + EXT, :] = packed
+
+
+def front_rows(j, dt_bias, decay_rate, skip_d, dt_rows):
+    scalar = pl.BlockSpec(memory_space=pltpu.SMEM)
+    return pl.pallas_call(
+        front_body,
+        in_specs=[scalar, scalar, scalar, scalar, pl.BlockSpec(memory_space=pltpu.VMEM)],
+        out_specs=pl.BlockSpec(memory_space=pltpu.VMEM),
+        out_shape=pltpu.HBM((GROUPS, dt_rows.shape[0] + EXT, 128), bf16),
+        compiler_params=params(8),
+        name="front_rows",
+    )(j.reshape(1), in_hbm(dt_bias), in_hbm(decay_rate), in_hbm(skip_d), in_hbm(dt_rows))
 
 
 def steps_body(meta_ref, dt_ref, par_ref, ein_ref, eout_ref, rows_ref):
     s = pl.program_id(0)
     z, j, length = meta_ref[0], meta_ref[1], meta_ref[2 + s]
-    par = jnp.sum(par_ref[...], axis=0)
-    bias, rate, skip = par[0:1], par[1:2], par[2:3]
     src = lax.broadcasted_iota(jnp.int32, (128, 128), 0)
     dst = lax.broadcasted_iota(jnp.int32, (128, 128), 1)
+    join = ((src & 15) == (dst & 15)) & (src < 48) & (dst < 48)
+    par = jnp.sum(par_ref[...].astype(f32), axis=0).astype(bf16)
+    par = dot(par, join.astype(f32).astype(bf16))
+    bias, rate, skip = par[0:1], par[1:2], par[2:3]
     sel = ((src == j * GROUP_HEADS + (dst & 15)) & (dst < 48)).astype(f32).astype(bf16)
-    raw = dot(dt_ref[...].reshape(SLAB, 128).astype(bf16), sel)
+    raw = dot(dt_ref[...].reshape(SLAB, 128), sel)
     pos = z * SLAB + lax.broadcasted_iota(jnp.int32, (SLAB, 128), 0)
     arg = raw + bias
     dt = jnp.maximum(arg, 0.0) + jnp.log1p(jnp.exp(-jnp.abs(arg)))
@@ -110,7 +161,7 @@
             grid=(seqs,),
             in_specs=[
                 pl.BlockSpec((GROUPS, ROWS, 128), lambda s, m: (0, s, 0)),
-                pl.BlockSpec((GROUPS, 8, 128), lambda s, m: (0, 0, 0)),
+                pl.BlockSpec((GROUPS, EXT, 128), lambda s, m: (0, 0, 0)),
             ],
             out_specs=[
                 pl.BlockSpec((1, SLAB, 128), lambda s, m: (s, 0, 0)),
@@ -123,12 +174,12 @@
             jax.ShapeDtypeStruct((seqs, SLAB, 128), bf16),
             jax.ShapeDtypeStruct((seqs, EXT, 128), bf16),
         ],
-        compiler_params=params(),
+        compiler_params=params(16),
         name="step_factors",
     )(meta, dt_all, par_all)
 
 
-def conv_body(first, meta_ref, recv_ref, halo_ref, w_ref, ein_ref, rows_ref, e3_ref, xbc_ref, sout_ref, xs):
+def conv_body(first, meta_ref, recv_ref, halo_ref, w_ref, ein_ref, rows_ref, e3_ref, xbc_ref, sout_ref, xs, scaled):
     s = pl.program_id(0)
     z, length = meta_ref[0], meta_ref[2 + first + s]
     xs[0:8, :] = halo_ref[0]
@@ -144,13 +195,15 @@
             acc = w_ref[3:4, lane : lane + 256] * win[8:]
             for back in (1, 2, 3):
                 acc = acc + w_ref[3 - back : 4 - back, lane : lane + 256] * pltpu.roll(win, back, 0)[8:]
-            xbc_ref[0, pl.ds(start, ROWS), lane : lane + 256] = jnp.where(keep, silu(acc), 0.0).astype(bf16)
+            xbc_ref[0, pl.ds(start, ROWS), lane : lane + 256] = jnp.where(keep, acc + acc * jnp.tanh(acc), 0.0).astype(bf16)
         return 0
 
     lax.fori_loop(0, GROUPS, per_rows, 0)
     e3 = e3_ref[...]
-    scaled = (xbc_ref[0, :, 0:GROUP_X].astype(f32) * dot(ein_ref[0], e3)).astype(bf16)
-    state = dot(xbc_ref[0, :, GROUP_X : GROUP_X + STATE], scaled, 0, 0)
+    for b in range(0, SLAB, 128):
+        here = slice(b, b + 128)
+        scaled[here] = (xbc_ref[0, here, 0:GROUP_X].astype(f32) * dot(ein_ref[0, here], e3)).astype(bf16)
+    state = dot(xbc_ref[0, :, GROUP_X : GROUP_X + STATE], scaled[...], 0, 0)
     grow = dot(rows_ref[0], e3)[0:1]
     state = (state * grow).astype(bf16)
     which = lax.broadcasted_iota(jnp.int32, (EXT, GROUP_X), 0)
@@ -179,15 +232,15 @@
                 pl.BlockSpec((1, SLAB, GROUP_CH), lambda s, m: (s, 0, 0)),
                 pl.BlockSpec((GROUPS, 1, STATE + EXT, 128), lambda s, m: (0, s, 0, 0)),
             ],
-            scratch_shapes=[pltpu.VMEM((SLAB + 8, GROUP_CH), f32)],
+            scratch_shapes=[pltpu.VMEM((SLAB + 8, GROUP_CH), f32), pltpu.VMEM((SLAB, GROUP_X), bf16)],
         ),
         out_shape=[
-            jax.ShapeDtypeStruct((count, SLAB, GROUP_CH), bf16),
-            jax.ShapeDtypeStruct((GROUPS, count, STATE + EXT, 128), bf16),
-        ],
-        compiler_params=params(),
+            pltpu.HBM((count, SLAB, GROUP_CH), bf16),
+            pltpu.HBM((GROUPS, count, STATE + EXT, 128), bf16),
+        ],
+        compiler_params=params(24),
         name="conv_and_state",
-    )(meta, recv, halo, weight, ein, rows, e3)
+    )(meta, in_hbm(recv), halo, weight, ein, rows, e3)
 
 
 def inner_body(xbc_ref, ein_ref, eout_ref, rows_ref, e3_ref, out_ref):
@@ -221,10 +274,10 @@
             pl.BlockSpec((128, GROUP_X), lambda s: (0, 0)),
         ],
         out_specs=pl.BlockSpec((1, SLAB, GROUP_X), lambda s: (s, 0, 0)),
-        out_shape=jax.ShapeDtypeStruct((count, SLAB, GROUP_X), f32),
-        compiler_params=params(),
+        out_shape=pltpu.HBM((count, SLAB, GROUP_X), f32),
+        compiler_params=params(24),
         name="inner_output",
-    )(xbc, ein, eout, rows, e3)
+    )(in_hbm(xbc), ein, eout, rows, e3)
 
 
 def scan_body(got_ref, seed_ref, start_ref, final_ref):
@@ -234,7 +287,7 @@
         extra = got_ref[k, 0, STATE : STATE + EXT, :].astype(f32)
         root = extra[0:1] + extra[1:2] + extra[2:3]
         state = (root * root) * state + got_ref[k, 0, 0:STATE, :].astype(f32)
-    final_ref[0] = state.T
+    final_ref[0] = state.T.astype(bf16)
 
 
 def scan_slabs(got, seed, first, count):
@@ -251,10 +304,10 @@
             pl.BlockSpec((1, 128, STATE), lambda s: (s, 0, 0)),
         ],
         out_shape=[
-            jax.ShapeDtypeStruct((slabs, count, STATE, 128), bf16),
-            jax.ShapeDtypeStruct((count, 128, STATE), f32),
-        ],
-        compiler_params=params(),
+            pltpu.HBM((slabs, count, STATE, 128), bf16),
+            jax.ShapeDtypeStruct((count, 128, STATE), bf16),
+        ],
+        compiler_params=params(12),
         name="scan_slabs",
     )(got, seed)
 
@@ -263,60 +316,70 @@
     e3 = e3_ref[...]
     grow = dot(rows_ref[0], e3)[0:1]
     state = jnp.concatenate([start_ref[k, 0] for k in range(GROUPS)], axis=1)
-    carried = dot(c_ref[0], state)
-    total = part_ref[0] + dot(eout_ref[0], e3) * grow * carried
-    for b in range(GROUPS):
-        out_ref[b, 0] = total[ROWS * b : ROWS * (b + 1)].astype(bf16)
+    for b in range(out_ref.shape[0]):
+        here = slice(ROWS * b, ROWS * (b + 1))
+        carried = dot(c_ref[0, here], state)
+        out_ref[b, 0] = (part_ref[0, here] + dot(eout_ref[0, here], e3) * (grow * carried)).astype(bf16)
 
 
 def finish_output(part, xbc, start, eout, rows, e3, first, count):
     c_at = GROUP_CH // STATE - 1
+    half = SLAB // 2
     return pl.pallas_call(
         finish_body,
-        grid=(count,),
+        grid=(count, 2),
         in_specs=[
-            pl.BlockSpec((1, SLAB, GROUP_X), lambda s: (s, 0, 0)),
-            pl.BlockSpec((1, SLAB, STATE), lambda s: (s, 0, c_at)),
-            pl.BlockSpec((GROUPS, 1, STATE, 128), lambda s: (0, s, 0, 0)),
-            pl.BlockSpec((1, SLAB, 128), lambda s: (first + s, 0, 0)),
-            pl.BlockSpec((1, EXT, 128), lambda s: (first + s, 0, 0)),
-            pl.BlockSpec((128, GROUP_X), lambda s: (0, 0)),
-        ],
-        out_specs=pl.BlockSpec((GROUPS, 1, ROWS, GROUP_X), lambda s: (0, s, 0, 0)),
-        out_shape=jax.ShapeDtypeStruct((GROUPS, count, ROWS, GROUP_X), bf16),
-        compiler_params=params(),
+            pl.BlockSpec((1, half, GROUP_X), lambda s, h: (s, h, 0)),
+            pl.BlockSpec((1, half, STATE), lambda s, h: (s, h, c_at)),
+            pl.BlockSpec((GROUPS, 1, STATE, 128), lambda s, h: (0, s, 0, 0)),
+            pl.BlockSpec((1, half, 128), lambda s, h: (first + s, h, 0)),
+            pl.BlockSpec((1, EXT, 128), lambda s, h: (first + s, 0, 0)),
+            pl.BlockSpec((128, GROUP_X), lambda s, h: (0, 0)),
+        ],
+        out_specs=pl.BlockSpec((GROUPS // 2, 1, ROWS, GROUP_X), lambda s, h: (h, s, 0, 0)),
+        out_shape=pltpu.HBM((GROUPS, count, ROWS, GROUP_X), bf16),
+        compiler_params=params(24),
         name="finish_output",
-    )(part, xbc, start, eout, rows, e3)
+    )(in_hbm(part), in_hbm(xbc), start, eout, rows, e3)
+
+
+PAIR = 2
 
 
 def norm_body(meta_ref, y_ref, gate_ref, gain_ref, out_ref):
     at = (meta_ref[0] * GROUPS + meta_ref[1]) * ROWS
-    gain = gain_ref[...]
-    for s in range(out_ref.shape[0]):
-        gated = y_ref[0, s].astype(f32) * silu(gate_ref[s].astype(f32))
-        mean = jnp.mean(gated * gated, axis=-1, keepdims=True)
-        pos = at + lax.broadcasted_iota(jnp.int32, (ROWS, 1), 0)
-        scale = jnp.where(pos < meta_ref[2 + s], lax.rsqrt(mean + norm_eps), 0.0)
-        out_ref[s] = (gated * scale * gain).astype(bf16)
+    step = 32
+    for q in range(PAIR):
+        lanes = slice(GROUP_X * q, GROUP_X * (q + 1))
+        gain = gain_ref[:, lanes]
+        for s in range(out_ref.shape[0]):
+            for row in range(0, ROWS, step):
+                here = slice(row, row + step)
+                gated = y_ref[q, s, here].astype(f32) * silu(gate_ref[s, here, lanes].astype(f32))
+                mean = jnp.mean(gated * gated, axis=-1, keepdims=True)
+                pos = at + row + lax.broadcasted_iota(jnp.int32, (step, 1), 0)
+                scale = jnp.where(pos < meta_ref[2 + s], lax.rsqrt(mean + norm_eps), 0.0)
+                out_ref[s, here, lanes] = (gated * scale * gain).astype(bf16)
 
 
 def gated_norm(meta, y, gate_z, gain, seqs):
+    width = PAIR * GROUP_X
     return pl.pallas_call(
         norm_body,
         grid_spec=pltpu.PrefetchScalarGridSpec(
             num_scalar_prefetch=1,
-            grid=(GROUPS,),
+            grid=(GROUPS // PAIR,),
             in_specs=[
-                pl.BlockSpec((1, seqs, ROWS, GROUP_X), lambda g, m: (g, 0, 0, 0)),
-                pl.BlockSpec((seqs, ROWS, GROUP_X), lambda g, m: (0, 0, g)),
-                pl.BlockSpec((1, GROUP_X), lambda g, m: (0, g)),
-            ],
-            out_specs=pl.BlockSpec((seqs, ROWS, GROUP_X), lambda g, m: (0, 0, g)),
+                pl.BlockSpec((PAIR, seqs, ROWS, GROUP_X), lambda g, m: (g, 0, 0, 0)),
+                pl.BlockSpec((seqs, ROWS, width), lambda g, m: (0, 0, g)),
+                pl.BlockSpec((1, width), lambda g, m: (0, g)),
+            ],
+            out_specs=pl.BlockSpec((seqs, ROWS, width), lambda g, m: (0, 0, g)),
         ),
-        out_shape=jax.ShapeDtypeStruct((seqs, ROWS, INNER), bf16),
-        compiler_params=params(),
+        out_shape=pltpu.HBM((seqs, ROWS, INNER), bf16),
+        compiler_params=params(20),
         name="gated_norm",
-    )(meta, y, gate_z, gain)
+    )(meta, in_hbm(y), gate_z, gain)
 
 
 def local(
@@ -354,43 +417,46 @@
             axis=-1,
         )
 
+    front = front_rows(j, dt_bias, decay_rate, skip_d, dt_raw.reshape(seqs * ROWS, 128))
+    front = lax.all_to_all(front, "j", 0, 0, tiled=True)
     sent = pack_groups(conv_input, 0, seqs)
+    sent, front = lax.optimization_barrier((sent, front))
     recv = lax.all_to_all(sent, "j", 0, 0, tiled=True)
 
     valid_len = lax.dynamic_slice_in_dim(lengths, first_seq, seqs)
     hit = lax.dynamic_slice_in_dim(prefix_hit, first_seq, seqs)
     owner = lax.dynamic_slice_in_dim(route_owner, first_seq, seqs)
     slot = lax.dynamic_slice_in_dim(route_slot, first_seq, seqs)
-    pick = owner * slot_count + slot
     meta = jnp.concatenate([jnp.stack([z, j]).astype(jnp.int32), valid_len])
 
-    whole_state = lax.all_gather(pool_state, "pool", axis=0, tiled=True)
-    seed = jnp.take(whole_state, pick, axis=0) * hit.astype(bf16)[:, None, None, None]
-    seed = lax.ppermute(seed.reshape(seqs, 128, STATE), ("z", "j"), flip)
-
-    whole_tail = lax.all_gather(group_columns(pool_tail), "pool", axis=0, tiled=True)
-    tail = jnp.take(whole_tail, pick, axis=0) * hit.astype(bf16)[:, None, None]
-
-    lane = jnp.arange(128, dtype=jnp.int32)
-    own = jnp.stack([dt_bias, decay_rate, skip_d])
-    here = (lane < 48) & ((lane & 15) // 2 == j)
-    par = jnp.where(here, jnp.where(lane & 1 == 0, own[:, 0:1], own[:, 1:2]), 0.0)
-    par = jnp.pad(par, ((0, 5), (0, 0)))
-    mine = jnp.concatenate([dt_raw.reshape(seqs * ROWS, 128).astype(f32), par], axis=0)
-    both = lax.all_gather(mine, "j", axis=0, tiled=False)
-    par_all = lax.ppermute(both[:, seqs * ROWS :], ("z", "j"), flip)
-    ein, eout, rows = step_factors(meta, both, par_all, seqs)
+    pools = lax.axis_size("pool")
+
+    def from_pools(mine):
+        parts = [mine]
+        for k in range(1, pools):
+            parts.append(lax.ppermute(mine, "pool", [(i, (i + k) % pools) for i in range(pools)]))
+        return jnp.concatenate(parts, axis=0)
+
+    par_all = lax.ppermute(front[:, seqs * ROWS :], ("z", "j"), flip)
+    mine, par_all = lax.optimization_barrier((pool_state.reshape(slot_count, 128, STATE), par_all))
+    pick = (lax.axis_index("pool") - owner) % pools * slot_count + slot
+    seed = jnp.take(from_pools(mine), pick, axis=0) * hit.astype(bf16)[:, None, None]
+    ein, eout, rows = step_factors(meta, front, par_all, seqs)
+    tails, seed, ein = lax.optimization_barrier((group_columns(pool_tail), seed, ein))
+    seed = lax.ppermute(seed, ("z", "j"), flip)
+    tail = jnp.take(from_pools(tails), pick, axis=0) * hit.astype(bf16)[:, None, None]
 
     head_of = jnp.arange(GROUP_X, dtype=jnp.int32)[None, :] // HEAD_DIM
     src = jnp.arange(128, dtype=jnp.int32)[:, None]
     e3 = ((src < 48) & ((src & 15) == head_of)).astype(bf16)
-    weight = group_columns(conv_weight)
+    weight = 0.5 * group_columns(conv_weight)
 
     before = lax.ppermute(recv[GROUPS - 1, :, ROWS - 3 :], "z", [(k, k + 1) for k in range(slabs - 1)])
     halo = jnp.where(z == 0, tail, before).astype(f32)
     halo = jnp.pad(halo, ((0, 0), (5, 0), (0, 0)))
 
     xbc, sout = conv_and_state(meta, recv, halo, weight, ein, rows, e3, 0, seqs)
+    sout, seed = lax.optimization_barrier((sout, seed))
     got = lax.all_to_all(sout, "z", 0, 0, tiled=True)
     part = inner_output(xbc, ein, eout, rows, e3, 0, seqs)
     start, final = scan_slabs(got, seed, 0, seqs)
@@ -399,7 +465,7 @@
     y = finish_output(part, xbc, back, eout, rows, e3, 0, seqs)
     token = lax.all_to_all(y, "j", 0, 0, tiled=True)
     mixed = gated_norm(meta, token, gate_z, norm_gain.reshape(1, INNER), seqs)
-    return (mixed, final.reshape(seqs, 2, HEAD_DIM, STATE))
+    return (mixed, final.astype(f32).reshape(seqs, 2, HEAD_DIM, STATE))
 
 
 def solution(mesh):

time: 250 us -> 208 us (0.83)
  blocking collectives: 64.6 us -> 37.1 us
  between operations: 14.3 us -> 0.9 us
  local copies, waits for them, and re-layouts: 15.6 us -> 5.82 us
  waiting for transfers between devices: 68.5 us -> 73.2 us
  Pallas kernels: 39.3 us -> 42.7 us
    all_gather x2 -> x0, blocking collectives: 64.6 us -> none  [the longest x1 54.1 us: local(): both = lax.all_gather(mine, 'j', axis=0, tiled=False)]
    all_to_all x0 -> x1, blocking collectives: none -> 37.1 us  [local(): got = lax.all_to_all(sout, 'z', 0, 0, tiled=True)]
    all_to_all x1, waiting for transfers between devices: 0.01 us -> 15.4 us  [local(): recv = lax.all_to_all(sent, 'j', 0, 0, tiled=True)]
    unnamed x31 -> x19, local copies, waits for them, and re-layouts: 9 us -> 0.8 us
    all_to_all x1, starting transfers between devices: 11.3 us -> 3.55 us  [local(): back = lax.all_to_all(start, 'z', 0, 0, tiled=True)]
    ppermute x2 -> x8, starting transfers between devices: 9.05 us -> 15.2 us  [the longest x6 8.49 us: from_pools(): lax.ppermute(mine, 'pool', [(i, (i + k) % pools) for i in range(pools)])]
    ppermute x2 -> x8, waiting for transfers between devices: 10.7 us -> 5.28 us  [the longest x6 2.75 us: from_pools(): lax.ppermute(mine, 'pool', [(i, (i + k) % pools) for i in range(pools)])]
    all_to_all x1, waiting for transfers between devices: 34.8 us -> 31.5 us  [local(): token = lax.all_to_all(y, 'j', 0, 0, tiled=True)]
  transfers between devices with their start and end apart: 9 -> 14, of which waited for: 5 -> 9; matrix products, arithmetic and copies ran while one was open for 3% -> 4% of each run, Pallas kernels for 8% -> 13%
where the time goes in v2:
time: 208 us; the launch traced here: 207 us
  waiting for transfers between devices  73.2 us (35%)
  starting transfers between devices  44.4 us (21%)
  Pallas kernels  42.7 us (21%)
  blocking collectives  37.1 us (18%)
  local copies, waits for them, and re-layouts  5.82 us (3%)
  other arithmetic  2.76 us (1%)
    all_to_all x1, blocking collectives, local(): got = lax.all_to_all(sout, 'z', 0, 0, tiled=True)  37.1 us
    all_to_all x1, waiting for transfers between devices, local(): token = lax.all_to_all(y, 'j', 0, 0, tiled=True)  31.5 us
    all_to_all x1, waiting for transfers between devices, local(): recv = lax.all_to_all(sent, 'j', 0, 0, tiled=True)  15.4 us
    all_to_all x1, waiting for transfers between devices, local(): back = lax.all_to_all(start, 'z', 0, 0, tiled=True)  12.3 us
    pallas_call x1, Pallas kernels, conv_and_state(): pl.pallas_call(functools.partial(conv_body, first), grid_spec=pltpu.Prefe...  10.4 us
    all_to_all x1, starting transfers between devices, local(): token = lax.all_to_all(y, 'j', 0, 0, tiled=True)  8.71 us
    ppermute x6, starting transfers between devices, from_pools(): lax.ppermute(mine, 'pool', [(i, (i + k) % pools) for i in range(pools)])  8.49 us
    pallas_call x1, Pallas kernels, inner_output(): pl.pallas_call(inner_body, grid=(count,), in_specs=[pl.BlockSpec((1, SLAB...  7.63 us
  transfers between devices with their start and end apart: 14, of which 9 were waited for; matrix products, arithmetic and copies ran while one was open for 4% of the time, Pallas kernels for 13%

profile of v2, /device:TPU:1, one launch (start us, length us, event | category | flops | bytes accessed | tf_op | source)
XLA Modules:
  0.0 206.9 jit_solution(3878503665420649481)
XLA Ops:
  0.6 1.6 front_rows.1
  2.3 6.6 %all-to-all-start = ((bf16[8,208,128]{2,1,0:T(8,128)(2,1)}), bf16[8,208,128]{2,1,0:T(8,128)(2,1)S(1)}, u32[]{:S(2)}, u32[]{:S(2)}) async-start(bf16[8,208,128]{2,1,0:T(8,128)(2,1)} %front_rows.1), calls=%async_computation | async-start | bytes 851968 | tf_op jit(solution)/shard_map/all_to_all | solution.py:421
  8.9 3.9 %pack_groups.1 = bf16[8,3,64,1280]{3,2,1,0:T(8,128)(2,1)} custom-call(bf16[3,64,10240]{2,1,0:T(8,128)(2,1)} %x_ref.1), custom_call_target="tpu_custom_call" | custom-call | tf_op jit(solution)/shard_map/pack_groups/pallas_call | solution.py:86
  12.8 0.0 copy-start.4
  12.8 0.0 copy-start.5
  12.8 0.0 copy-start.6
  12.9 0.0 copy-start.7
  12.9 0.0 copy-start.2
  12.9 4.4 %all-to-all-done.dt_ref = bf16[8,208,128]{2,1,0:T(8,128)(2,1)S(1)} async-done(((bf16[8,208,128]{2,1,0:T(8,128)(2,1)}), bf16[8,208,128]{2,1,0:T(8,128)(2,1)S(1)}, u32[]{:S(2)}, u32[]{:S(2)}) %all-to-all-start) | async-done | bytes 426016 | tf_op jit(solution)/shard_map/all_to_all | solution.py:421
  17.3 5.3 %all-to-all-start.1 = ((bf16[8,3,64,1280]{3,2,1,0:T(8,128)(2,1)}), bf16[8,3,64,1280]{3,2,1,0:T(8,128)(2,1)}, u32[]{:S(2)}, u32[]{:S(2)}) async-start(bf16[8,3,64,1280]{3,2,1,0:T(8,128)(2,1)} %pack_groups.1), calls=%async_computation.1 | async-start | bytes 7864320 | tf_op jit(solution)/shard_map/all_to_all | solution.py:424
  22.6 0.7 constant_dynamic-slice_fusion.4
  23.3 0.8 constant_dynamic-slice_fusion.5
  24.2 0.0 copy-done.4
  24.2 0.0 copy-done.5
  24.2 0.1 compare_and_fusion
  24.3 0.7 constant_dynamic-slice_fusion.1
  25.0 0.7 constant_dynamic-slice_fusion.2
  25.8 2.9 %collective-permute-start = (bf16[8,16,128]{2,1,0:T(8,128)(2,1)S(1)}, bf16[8,16,128]{2,1,0:T(8,128)(2,1)S(1)}, u32[]{:S(2)}, u32[]{:S(2)}) collective-permute-start(bf16[8,16,128]{2,1,0:T(8,128)(2,1)S(1)} %slice.6), channel_id=1, source_target_pairs={{0,0},{4,32},{8,64},{12,96},{16,128},{20,160},{24,192},{28,224},{3... | collective-permute-start | bytes 98312 | tf_op jit(solution)/shard_map/ppermute | solution.py:440
  28.8 0.0 copy-done.6
  28.8 0.1 dynamic-slice_convert_fusion
  28.9 0.0 copy-done.7
  28.9 0.1 dynamic_slice.30
  28.9 2.5 %collective-permute-done.par_ref = bf16[8,16,128]{2,1,0:T(8,128)(2,1)S(1)} collective-permute-done((bf16[8,16,128]{2,1,0:T(8,128)(2,1)S(1)}, bf16[8,16,128]{2,1,0:T(8,128)(2,1)S(1)}, u32[]{:S(2)}, u32[]{:S(2)}) %collective-permute-start) | collective-permute-done | bytes 32800 | tf_op jit(solution)/shard_map/ppermute | solution.py:440
  31.5 0.6 collective-permute-start.1
  32.0 2.5 %collective-permute-start.2 = (bf16[8,128,128]{2,1,0:T(8,128)(2,1)S(1)}, bf16[8,128,128]{2,1,0:T(8,128)(2,1)S(1)}, u32[]{:S(2)}, u32[]{:S(2)}) collective-permute-start(bf16[8,128,128]{2,1,0:T(8,128)(2,1)S(1)} %bitcast.11), channel_id=1, source_target_pairs={{0,2},{1,3},{2,0},{3,1},{4,6},{5,7},{6,4},{7,5},{8,10},{9,11},{10,... | collective-permute-start | bytes 786440 | tf_op jit(solution)/shard_map/ppermute | solution.py:437
  34.5 1.2 collective-permute-start.3
  35.6 0.1 pad_add_fusion.meta_ref
  35.7 0.1 and_convert_fusion.e3_ref
  35.9 4.1 %step_factors.1 = (bf16[3,512,128]{2,1,0:T(8,128)(2,1)S(1)}, bf16[3,512,128]{2,1,0:T(8,128)(2,1)S(1)}, bf16[3,16,128]{2,1,0:T(8,128)(2,1)S(1)}) custom-call(s32[5]{0:T(128)S(1)} %pad_add_fusion.meta_ref, bf16[8,208,128]{2,1,0:T(8,128)(2,1)S(1)} %all-to-all-done.dt_ref, bf16[8,16,128]{2,1,0:T(8,128)(2,1)S(1)} %collective-permute-done.par_ref), custom_call_target="tpu_custom_call" | custom-call | tf_op jit(solution)/shard_map/step_factors/pallas_call | solution.py:157
  40.0 0.0 collective-permute-done.1
  40.0 2.5 %collective-permute-done.2 = bf16[8,128,128]{2,1,0:T(8,128)(2,1)S(1)} collective-permute-done((bf16[8,128,128]{2,1,0:T(8,128)(2,1)S(1)}, bf16[8,128,128]{2,1,0:T(8,128)(2,1)S(1)}, u32[]{:S(2)}, u32[]{:S(2)}) %collective-permute-start.2) | collective-permute-done | bytes 262176 | tf_op jit(solution)/shard_map/ppermute | solution.py:437
  42.5 0.7 copy-done.3
  43.2 0.2 collective-permute-done.3
  43.4 1.2 pad_maximum_fusion
  44.6 0.6 gather_fusion
  45.2 0.1 select_multiply_fusion
  45.3 1.6 collective-permute-start.4
  46.8 2.1 %collective-permute-start.5 = (bf16[8,3,1280]{2,1,0:T(4,128)(2,1)S(1)}, bf16[8,3,1280]{2,1,0:T(4,128)(2,1)S(1)}, u32[]{:S(2)}, u32[]{:S(2)}) collective-permute-start(bf16[8,3,1280]{2,1,0:T(4,128)(2,1)S(1)} %pad_maximum_fusion.2), channel_id=1, source_target_pairs={{0,2},{1,3},{2,0},{3,1},{4,6},{5,7},{6,4},{7,5},{8,10},{9,11},{10,... | collective-permute-start | bytes 184328 | tf_op jit(solution)/shard_map/ppermute | solution.py:437
  48.9 0.7 collective-permute-start.6
  49.6 3.8 %collective-permute-start.8 = (bf16[3,128,128]{2,1,0:T(8,128)(2,1)S(1)}, bf16[3,128,128]{2,1,0:T(8,128)(2,1)S(1)}, u32[]{:S(2)}, u32[]{:S(2)}) collective-permute-start(bf16[3,128,128]{2,1,0:T(8,128)(2,1)S(1)} %select_multiply_fusion), channel_id=1, source_target_pairs={{0,0},{4,32},{8,64},{12,96},{16,128},{20,160},{24,192},{28,224},{3... | collective-permute-start | bytes 294920 | tf_op jit(solution)/shard_map/ppermute | solution.py:446
  53.4 15.4 %all-to-all-done.1.recv_ref = bf16[8,3,64,1280]{3,2,1,0:T(8,128)(2,1)} async-done(((bf16[8,3,64,1280]{3,2,1,0:T(8,128)(2,1)}), bf16[8,3,64,1280]{3,2,1,0:T(8,128)(2,1)}, u32[]{:S(2)}, u32[]{:S(2)}) %all-to-all-start.1) | async-done | bytes 3932192 | tf_op jit(solution)/shard_map/all_to_all | solution.py:424
  68.8 0.8 slice_bitcast_fusion
  69.7 2.9 %collective-permute-start.7 = (bf16[3,3,1280]{2,1,0:T(4,128)(2,1)S(1)}, bf16[3,3,1280]{2,1,0:T(4,128)(2,1)S(1)}, u32[]{:S(2)}, u32[]{:S(2)}) collective-permute-start(bf16[3,3,1280]{2,1,0:T(4,128)(2,1)S(1)} %slice_bitcast_fusion), channel_id=1, source_target_pairs={{0,32},{32,64},{64,96},{96,128},{128,160},{160,192},{192,224},{1,3... | collective-permute-start | bytes 69128 | tf_op jit(solution)/shard_map/ppermute | solution.py:454
  72.6 0.0 collective-permute-done.4
  72.6 0.0 collective-permute-done.5
  72.6 0.0 collective-permute-done.6
  72.6 0.2 pad_maximum_fusion.1
  72.8 0.6 gather_fusion.1
  73.4 0.1 collective-permute-done.7
  73.5 0.1 multiply_select_fusion
  73.7 10.4 %conv_and_state.1 = (bf16[3,512,1280]{2,1,0:T(8,128)(2,1)}, bf16[8,3,144,128]{3,2,1,0:T(8,128)(2,1)}) custom-call(s32[5]{0:T(128)S(1)} %pad_add_fusion.meta_ref, bf16[8,3,64,1280]{3,2,1,0:T(8,128)(2,1)} %all-to-all-done.1.recv_ref, f32[3,8,1280]{2,1,0:T(8,128)S(1)} %pad_convert_fusion.halo_ref, f32[4,1280]{1,0:T(4,128)S(1)} %maximum_multiply_fusion.w_ref, ...), custom_call_target="tpu_custom_call" | custom-call | tf_op jit(solution)/shard_map/conv_and_state/pallas_call | solution.py:218
  84.0 0.0 collective-permute-done.8.seed_ref
  84.0 37.1 %all_to_all.25.got_ref = bf16[8,3,144,128]{3,2,1,0:T(8,128)(2,1)S(1)} all-to-all(bf16[8,3,144,128]{3,2,1,0:T(8,128)(2,1)} %get-tuple-element.30), channel_id=1, replica_groups=mesh['z'=8,'j'=8,'pool'=4] {'z'}, dimensions={0} | all-to-all | bytes 1769472 | tf_op jit(solution)/shard_map/all_to_all | solution.py:460
  121.1 1.9 scan_slabs.1
  123.0 3.5 %all-to-all-start.3 = ((bf16[8,3,128,128]{3,2,1,0:T(8,128)(2,1)}), bf16[8,3,128,128]{3,2,1,0:T(8,128)(2,1)S(1)}, u32[]{:S(2)}, u32[]{:S(2)}) async-start(bf16[8,3,128,128]{3,2,1,0:T(8,128)(2,1)} %get-tuple-element.32), calls=%async_computation.3 | async-start | bytes 1572864 | tf_op jit(solution)/shard_map/all_to_all | solution.py:463
  126.6 7.6 %inner_output.1.part_ref = f32[3,512,1024]{2,1,0:T(8,128)} custom-call(bf16[3,512,1280]{2,1,0:T(8,128)(2,1)} %get-tuple-element.26.xbc_ref.c_ref, bf16[3,512,128]{2,1,0:T(8,128)(2,1)S(1)} %get-tuple-element.24.ein_ref, bf16[3,512,128]{2,1,0:T(8,128)(2,1)S(1)} %get-tuple-element.27.eout_ref, bf16[3,16,128]{2,1,0:T(8,128)(2,1)S(1)} %get-tuple-element.25.rows_ref, ...), custom_call_target="tpu_custom_call" | custom-call | tf_op jit(solution)/shard_map/inner_output/pallas_call | solution.py:266
  134.2 12.3 %all-to-all-done.3.start_ref = bf16[8,3,128,128]{3,2,1,0:T(8,128)(2,1)S(1)} async-done(((bf16[8,3,128,128]{3,2,1,0:T(8,128)(2,1)}), bf16[8,3,128,128]{3,2,1,0:T(8,128)(2,1)S(1)}, u32[]{:S(2)}, u32[]{:S(2)}) %all-to-all-start.3) | async-done | bytes 786464 | tf_op jit(solution)/shard_map/all_to_all | solution.py:463
  146.5 7.0 %finish_output.1 = bf16[8,3,64,1024]{3,2,1,0:T(8,128)(2,1)} custom-call(f32[3,512,1024]{2,1,0:T(8,128)} %inner_output.1.part_ref, bf16[3,512,1280]{2,1,0:T(8,128)(2,1)} %get-tuple-element.26.xbc_ref.c_ref, bf16[8,3,128,128]{3,2,1,0:T(8,128)(2,1)S(1)} %all-to-all-done.3.start_ref, bf16[3,512,128]{2,1,0:T(8,128)(2,1)S(1)} %get-tuple-element.27.eout_ref, ...), custom_call_target="tpu_custom_call" | custom-call | tf_op jit(solution)/shard_map/finish_output/pallas_call | solution.py:328
  153.5 8.7 %all-to-all-start.4 = ((bf16[8,3,64,1024]{3,2,1,0:T(8,128)(2,1)}), bf16[8,3,64,1024]{3,2,1,0:T(8,128)(2,1)}, u32[]{:S(2)}, u32[]{:S(2)}) async-start(bf16[8,3,64,1024]{3,2,1,0:T(8,128)(2,1)} %finish_output.1), calls=%async_computation.4 | async-start | bytes 6291456 | tf_op jit(solution)/shard_map/all_to_all | solution.py:466
  162.2 2.2 %collective-permute-start.9 = (bf16[3,128,128]{2,1,0:T(8,128)(2,1)S(1)}, bf16[3,128,128]{2,1,0:T(8,128)(2,1)S(1)}, u32[]{:S(2)}, u32[]{:S(2)}) collective-permute-start(bf16[3,128,128]{2,1,0:T(8,128)(2,1)S(1)} %get-tuple-element.33), channel_id=1, source_target_pairs={{0,0},{4,32},{8,64},{12,96},{16,128},{20,160},{24,192},{28,224},{3... | collective-permute-start | bytes 294920 | tf_op jit(solution)/shard_map/ppermute | solution.py:464
  164.4 4.1 %collective-permute-done.9 = bf16[3,128,128]{2,1,0:T(8,128)(2,1)S(1)} collective-permute-done((bf16[3,128,128]{2,1,0:T(8,128)(2,1)S(1)}, bf16[3,128,128]{2,1,0:T(8,128)(2,1)S(1)}, u32[]{:S(2)}, u32[]{:S(2)}) %collective-permute-start.9) | collective-permute-done | bytes 98336 | tf_op jit(solution)/shard_map/ppermute | solution.py:464
  168.6 0.7 convert.3
  169.3 31.5 %all-to-all-done.4.y_ref = bf16[8,3,64,1024]{3,2,1,0:T(8,128)(2,1)} async-done(((bf16[8,3,64,1024]{3,2,1,0:T(8,128)(2,1)}), bf16[8,3,64,1024]{3,2,1,0:T(8,128)(2,1)}, u32[]{:S(2)}, u32[]{:S(2)}) %all-to-all-start.4) | async-done | bytes 3145760 | tf_op jit(solution)/shard_map/all_to_all | solution.py:466
  200.7 6.1 %gated_norm.1 = bf16[3,64,8192]{2,1,0:T(8,128)(2,1)} custom-call(s32[5]{0:T(128)S(1)} %pad_add_fusion.meta_ref, bf16[8,3,64,1024]{3,2,1,0:T(8,128)(2,1)} %all-to-all-done.4.y_ref, bf16[3,64,8192]{2,1,0:T(8,128)(2,1)S(1)} %copy-done, f32[1,8192]{1,0:T(1,128)S(1)} %bitcast.9), custom_call_target="tpu_custom_call" | custom-call | tf_op jit(solution)/shard_map/gated_norm/pallas_call | solution.py:367
  (17 shorter events, 0.2 us)
Async XLA Ops:
  2.3 15.1 %all-to-all-start = ((bf16[8,208,128]{2,1,0:T(8,128)(2,1)}), bf16[8,208,128]{2,1,0:T(8,128)(2,1)S(1)}, u32[]{:S(2)}, u32[]{:S(2)}) async-start(bf16[8,208,128]{2,1,0:T(8,128)(2,1)} %front_rows.1), calls=%async_computation | async-start | bytes 851968 | tf_op jit(solution)/shard_map/all_to_all | solution.py:421
  12.8 11.4 %copy-start.4 = (s32[12]{0:T(128)S(1)}, s32[12]{0:T(128)}, u32[]{:S(2)}) copy-start(s32[12]{0:T(128)} %param.25) | copy-start | bytes 148
  12.8 11.4 %copy-start.5 = (s32[12]{0:T(128)S(1)}, s32[12]{0:T(128)}, u32[]{:S(2)}) copy-start(s32[12]{0:T(128)} %param.24) | copy-start | bytes 148
  12.8 15.9 %copy-start.6 = (s32[12]{0:T(128)S(1)}, s32[12]{0:T(128)}, u32[]{:S(2)}) copy-start(s32[12]{0:T(128)} %param.26) | copy-start | bytes 148
  12.9 16.0 %copy-start.7 = (s32[12]{0:T(128)S(1)}, s32[12]{0:T(128)}, u32[]{:S(2)}) copy-start(s32[12]{0:T(128)} %param.27) | copy-start | bytes 148
  12.9 18.6 %copy-start.2 = (bf16[8,2,64,128]{3,2,1,0:T(8,128)(2,1)S(1)}, bf16[8,2,64,128]{3,2,1,0:T(8,128)(2,1)}, u32[]{:S(2)}) copy-start(bf16[8,2,64,128]{3,2,1,0:T(8,128)(2,1)} %param.22) | copy-start | bytes 786436
  17.3 51.5 %all-to-all-start.1 = ((bf16[8,3,64,1280]{3,2,1,0:T(8,128)(2,1)}), bf16[8,3,64,1280]{3,2,1,0:T(8,128)(2,1)}, u32[]{:S(2)}, u32[]{:S(2)}) async-start(bf16[8,3,64,1280]{3,2,1,0:T(8,128)(2,1)} %pack_groups.1), calls=%async_computation.1 | async-start | bytes 7864320 | tf_op jit(solution)/shard_map/all_to_all | solution.py:424
  25.8 5.6 %collective-permute-start = (bf16[8,16,128]{2,1,0:T(8,128)(2,1)S(1)}, bf16[8,16,128]{2,1,0:T(8,128)(2,1)S(1)}, u32[]{:S(2)}, u32[]{:S(2)}) collective-permute-start(bf16[8,16,128]{2,1,0:T(8,128)(2,1)S(1)} %slice.6), channel_id=1, source_target_pairs={{0,0},{4,32},{8,64},{12,96},{16,128},{20,160},{24,192},{28,224},{3... | collective-permute-start | bytes 98312 | tf_op jit(solution)/shard_map/ppermute | solution.py:440
  31.5 8.5 %collective-permute-start.1 = (bf16[8,128,128]{2,1,0:T(8,128)(2,1)S(1)}, bf16[8,128,128]{2,1,0:T(8,128)(2,1)S(1)}, u32[]{:S(2)}, u32[]{:S(2)}) collective-permute-start(bf16[8,128,128]{2,1,0:T(8,128)(2,1)S(1)} %bitcast.10), channel_id=1, source_target_pairs={{0,1},{1,2},{2,3},{3,0},{4,5},{5,6},{6,7},{7,4},{8,9},{9,10},{10,1... | collective-permute-start | bytes 786440 | tf_op jit(solution)/shard_map/ppermute | solution.py:437
  32.0 10.5 %collective-permute-start.2 = (bf16[8,128,128]{2,1,0:T(8,128)(2,1)S(1)}, bf16[8,128,128]{2,1,0:T(8,128)(2,1)S(1)}, u32[]{:S(2)}, u32[]{:S(2)}) collective-permute-start(bf16[8,128,128]{2,1,0:T(8,128)(2,1)S(1)} %bitcast.11), channel_id=1, source_target_pairs={{0,2},{1,3},{2,0},{3,1},{4,6},{5,7},{6,4},{7,5},{8,10},{9,11},{10,... | collective-permute-start | bytes 786440 | tf_op jit(solution)/shard_map/ppermute | solution.py:437
  34.5 9.0 %collective-permute-start.3 = (bf16[8,128,128]{2,1,0:T(8,128)(2,1)S(1)}, bf16[8,128,128]{2,1,0:T(8,128)(2,1)}, u32[]{:S(2)}, u32[]{:S(2)}) collective-permute-start(bf16[8,128,128]{2,1,0:T(8,128)(2,1)S(1)} %bitcast.12), channel_id=1, source_target_pairs={{0,3},{1,0},{2,1},{3,2},{4,7},{5,4},{6,5},{7,6},{8,11},{9,8},{10,9... | collective-permute-start | bytes 786440 | tf_op jit(solution)/shard_map/ppermute | solution.py:437
  42.5 0.7 copy-start.3
  45.3 27.3 %collective-permute-start.4 = (bf16[8,3,1280]{2,1,0:T(4,128)(2,1)S(1)}, bf16[8,3,1280]{2,1,0:T(4,128)(2,1)S(1)}, u32[]{:S(2)}, u32[]{:S(2)}) collective-permute-start(bf16[8,3,1280]{2,1,0:T(4,128)(2,1)S(1)} %pad_maximum_fusion.2), channel_id=1, source_target_pairs={{0,1},{1,2},{2,3},{3,0},{4,5},{5,6},{6,7},{7,4},{8,9},{9,10},{10,1... | collective-permute-start | bytes 184328 | tf_op jit(solution)/shard_map/ppermute | solution.py:437
  46.8 25.7 %collective-permute-start.5 = (bf16[8,3,1280]{2,1,0:T(4,128)(2,1)S(1)}, bf16[8,3,1280]{2,1,0:T(4,128)(2,1)S(1)}, u32[]{:S(2)}, u32[]{:S(2)}) collective-permute-start(bf16[8,3,1280]{2,1,0:T(4,128)(2,1)S(1)} %pad_maximum_fusion.2), channel_id=1, source_target_pairs={{0,2},{1,3},{2,0},{3,1},{4,6},{5,7},{6,4},{7,5},{8,10},{9,11},{10,... | collective-permute-start | bytes 184328 | tf_op jit(solution)/shard_map/ppermute | solution.py:437
  48.9 23.7 %collective-permute-start.6 = (bf16[8,3,1280]{2,1,0:T(4,128)(2,1)S(1)}, bf16[8,3,1280]{2,1,0:T(4,128)(2,1)S(1)}, u32[]{:S(2)}, u32[]{:S(2)}) collective-permute-start(bf16[8,3,1280]{2,1,0:T(4,128)(2,1)S(1)} %pad_maximum_fusion.2), channel_id=1, source_target_pairs={{0,3},{1,0},{2,1},{3,2},{4,7},{5,4},{6,5},{7,6},{8,11},{9,8},{10,9... | collective-permute-start | bytes 184328 | tf_op jit(solution)/shard_map/ppermute | solution.py:437
  49.6 34.4 %collective-permute-start.8 = (bf16[3,128,128]{2,1,0:T(8,128)(2,1)S(1)}, bf16[3,128,128]{2,1,0:T(8,128)(2,1)S(1)}, u32[]{:S(2)}, u32[]{:S(2)}) collective-permute-start(bf16[3,128,128]{2,1,0:T(8,128)(2,1)S(1)} %select_multiply_fusion), channel_id=1, source_target_pairs={{0,0},{4,32},{8,64},{12,96},{16,128},{20,160},{24,192},{28,224},{3... | collective-permute-start | bytes 294920 | tf_op jit(solution)/shard_map/ppermute | solution.py:446
  69.7 3.9 %collective-permute-start.7 = (bf16[3,3,1280]{2,1,0:T(4,128)(2,1)S(1)}, bf16[3,3,1280]{2,1,0:T(4,128)(2,1)S(1)}, u32[]{:S(2)}, u32[]{:S(2)}) collective-permute-start(bf16[3,3,1280]{2,1,0:T(4,128)(2,1)S(1)} %slice_bitcast_fusion), channel_id=1, source_target_pairs={{0,32},{32,64},{64,96},{96,128},{128,160},{160,192},{192,224},{1,3... | collective-permute-start | bytes 69128 | tf_op jit(solution)/shard_map/ppermute | solution.py:454
  123.0 23.5 %all-to-all-start.3 = ((bf16[8,3,128,128]{3,2,1,0:T(8,128)(2,1)}), bf16[8,3,128,128]{3,2,1,0:T(8,128)(2,1)S(1)}, u32[]{:S(2)}, u32[]{:S(2)}) async-start(bf16[8,3,128,128]{3,2,1,0:T(8,128)(2,1)} %get-tuple-element.32), calls=%async_computation.3 | async-start | bytes 1572864 | tf_op jit(solution)/shard_map/all_to_all | solution.py:463
  153.5 47.2 %copy-start = (bf16[3,64,8192]{2,1,0:T(8,128)(2,1)S(1)}, bf16[3,64,8192]{2,1,0:T(8,128)(2,1)}, u32[]{:S(2)}) copy-start(bf16[3,64,8192]{2,1,0:T(8,128)(2,1)} %gate_ref.1) | copy-start | bytes 9437188
  153.5 47.2 %copy-start.1 = (f32[8192]{0:T(1024)S(1)}, f32[8192]{0:T(1024)}, u32[]{:S(2)}) copy-start(f32[8192]{0:T(1024)} %param.21) | copy-start | bytes 98308
  153.5 47.2 %all-to-all-start.4 = ((bf16[8,3,64,1024]{3,2,1,0:T(8,128)(2,1)}), bf16[8,3,64,1024]{3,2,1,0:T(8,128)(2,1)}, u32[]{:S(2)}, u32[]{:S(2)}) async-start(bf16[8,3,64,1024]{3,2,1,0:T(8,128)(2,1)} %finish_output.1), calls=%async_computation.4 | async-start | bytes 6291456 | tf_op jit(solution)/shard_map/all_to_all | solution.py:466
  162.2 6.3 %collective-permute-start.9 = (bf16[3,128,128]{2,1,0:T(8,128)(2,1)S(1)}, bf16[3,128,128]{2,1,0:T(8,128)(2,1)S(1)}, u32[]{:S(2)}, u32[]{:S(2)}) collective-permute-start(bf16[3,128,128]{2,1,0:T(8,128)(2,1)S(1)} %get-tuple-element.33), channel_id=1, source_target_pairs={{0,0},{4,32},{8,64},{12,96},{16,128},{20,160},{24,192},{28,224},{3... | collective-permute-start | bytes 294920 | tf_op jit(solution)/shard_map/ppermute | solution.py:464

commit v3 on v2

--- a/solution.py
+++ b/solution.py
@@ -179,10 +179,17 @@
     )(meta, dt_all, par_all)
 
 
-def conv_body(first, meta_ref, recv_ref, halo_ref, w_ref, ein_ref, rows_ref, e3_ref, xbc_ref, sout_ref, xs, scaled):
+def conv_rows(w_ref, lane, win):
+    acc = w_ref[3:4, lane : lane + 256] * win[8:]
+    for back in (1, 2, 3):
+        acc = acc + w_ref[3 - back : 4 - back, lane : lane + 256] * pltpu.roll(win, back, 0)[8:]
+    return acc + acc * jnp.tanh(acc)
+
+
+def conv_body(first, meta_ref, recv_ref, w_ref, xbc_ref, xs):
     s = pl.program_id(0)
     z, length = meta_ref[0], meta_ref[2 + first + s]
-    xs[0:8, :] = halo_ref[0]
+    xs[0:8, :] = jnp.zeros((8, GROUP_CH), f32)
     for b in range(GROUPS):
         xs[8 + ROWS * b : 8 + ROWS * (b + 1), :] = recv_ref[b, 0].astype(f32)
 
@@ -191,19 +198,50 @@
         pos = z * SLAB + start + lax.broadcasted_iota(jnp.int32, (ROWS, 256), 0)
         keep = pos < length
         for lane in range(0, GROUP_CH, 256):
-            win = xs[pl.ds(start, ROWS + 8), lane : lane + 256]
-            acc = w_ref[3:4, lane : lane + 256] * win[8:]
-            for back in (1, 2, 3):
-                acc = acc + w_ref[3 - back : 4 - back, lane : lane + 256] * pltpu.roll(win, back, 0)[8:]
-            xbc_ref[0, pl.ds(start, ROWS), lane : lane + 256] = jnp.where(keep, acc + acc * jnp.tanh(acc), 0.0).astype(bf16)
+            rows = conv_rows(w_ref, lane, xs[pl.ds(start, ROWS + 8), lane : lane + 256])
+            xbc_ref[0, pl.ds(start, ROWS), lane : lane + 256] = jnp.where(keep, rows, 0.0).astype(bf16)
         return 0
 
     lax.fori_loop(0, GROUPS, per_rows, 0)
+
+
+def conv_slab(meta, recv, weight, first, count):
+    return pl.pallas_call(
+        functools.partial(conv_body, first),
+        grid_spec=pltpu.PrefetchScalarGridSpec(
+            num_scalar_prefetch=1,
+            grid=(count,),
+            in_specs=[
+                pl.BlockSpec((GROUPS, 1, ROWS, GROUP_CH), lambda s, m: (0, s, 0, 0)),
+                pl.BlockSpec((4, GROUP_CH), lambda s, m: (0, 0)),
+            ],
+            out_specs=pl.BlockSpec((1, SLAB, GROUP_CH), lambda s, m: (s, 0, 0)),
+            scratch_shapes=[pltpu.VMEM((SLAB + 8, GROUP_CH), f32)],
+        ),
+        out_shape=pltpu.HBM((count, SLAB, GROUP_CH), bf16),
+        compiler_params=params(24),
+        name="conv_slab",
+    )(meta, in_hbm(recv), weight)
+
+
+def edge_body(first, meta_ref, xbc_ref, raw_ref, halo_ref, w_ref, ein_ref, rows_ref, e3_ref, edge_ref, sout_ref, scaled):
+    s = pl.program_id(0)
+    z, length = meta_ref[0], meta_ref[2 + first + s]
+    keep = z * SLAB + lax.broadcasted_iota(jnp.int32, (EXT, 256), 0) < length
+    for lane in range(0, GROUP_CH, 256):
+        lanes = slice(lane, lane + 256)
+        win = jnp.concatenate([halo_ref[0, :, lanes], raw_ref[0, 0, :, lanes].astype(f32)], axis=0)
+        edge_ref[0, :, lanes] = jnp.where(keep, conv_rows(w_ref, lane, win), 0.0).astype(bf16)
     e3 = e3_ref[...]
     for b in range(0, SLAB, 128):
         here = slice(b, b + 128)
-        scaled[here] = (xbc_ref[0, here, 0:GROUP_X].astype(f32) * dot(ein_ref[0, here], e3)).astype(bf16)
-    state = dot(xbc_ref[0, :, GROUP_X : GROUP_X + STATE], scaled[...], 0, 0)
+        x = xbc_ref[0, here, 0:GROUP_X]
+        if b == 0:
+            x = jnp.concatenate([edge_ref[0, :, 0:GROUP_X], x[EXT:]], axis=0)
+        scaled[here] = (x.astype(f32) * dot(ein_ref[0, here], e3)).astype(bf16)
+    b_lanes = slice(GROUP_X, GROUP_X + STATE)
+    b_all = jnp.concatenate([edge_ref[0, :, b_lanes], xbc_ref[0, EXT:, b_lanes]], axis=0)
+    state = dot(b_all, scaled[...], 0, 0)
     grow = dot(rows_ref[0], e3)[0:1]
     state = (state * grow).astype(bf16)
     which = lax.broadcasted_iota(jnp.int32, (EXT, GROUP_X), 0)
@@ -214,14 +252,15 @@
         sout_ref[k, 0, STATE : STATE + EXT, :] = extra[:, 128 * k : 128 * (k + 1)]
 
 
-def conv_and_state(meta, recv, halo, weight, ein, rows, e3, first, count):
-    return pl.pallas_call(
-        functools.partial(conv_body, first),
+def edge_and_state(meta, xbc, recv, halo, weight, ein, rows, e3, first, count):
+    return pl.pallas_call(
+        functools.partial(edge_body, first),
         grid_spec=pltpu.PrefetchScalarGridSpec(
             num_scalar_prefetch=1,
             grid=(count,),
             in_specs=[
-                pl.BlockSpec((GROUPS, 1, ROWS, GROUP_CH), lambda s, m: (0, s, 0, 0)),
+                pl.BlockSpec((1, SLAB, GROUP_CH), lambda s, m: (s, 0, 0)),
+                pl.BlockSpec((1, 1, EXT, GROUP_CH), lambda s, m: (0, s, 0, 0)),
                 pl.BlockSpec((1, 8, GROUP_CH), lambda s, m: (s, 0, 0)),
                 pl.BlockSpec((4, GROUP_CH), lambda s, m: (0, 0)),
                 pl.BlockSpec((1, SLAB, 128), lambda s, m: (first + s, 0, 0)),
@@ -229,18 +268,19 @@
                 pl.BlockSpec((128, GROUP_X), lambda s, m: (0, 0)),
             ],
             out_specs=[
-                pl.BlockSpec((1, SLAB, GROUP_CH), lambda s, m: (s, 0, 0)),
+                pl.BlockSpec((1, EXT, GROUP_CH), lambda s, m: (s, 0, 0)),
                 pl.BlockSpec((GROUPS, 1, STATE + EXT, 128), lambda s, m: (0, s, 0, 0)),
             ],
-            scratch_shapes=[pltpu.VMEM((SLAB + 8, GROUP_CH), f32), pltpu.VMEM((SLAB, GROUP_X), bf16)],
+            scratch_shapes=[pltpu.VMEM((SLAB, GROUP_X), bf16)],
         ),
         out_shape=[
             pltpu.HBM((count, SLAB, GROUP_CH), bf16),
             pltpu.HBM((GROUPS, count, STATE + EXT, 128), bf16),
         ],
+        input_output_aliases={1: 0},
         compiler_params=params(24),
-        name="conv_and_state",
-    )(meta, in_hbm(recv), halo, weight, ein, rows, e3)
+        name="edge_and_state",
+    )(meta, in_hbm(xbc), in_hbm(recv), halo, weight, ein, rows, e3)
 
 
 def inner_body(xbc_ref, ein_ref, eout_ref, rows_ref, e3_ref, out_ref):
@@ -455,7 +495,8 @@
     halo = jnp.where(z == 0, tail, before).astype(f32)
     halo = jnp.pad(halo, ((0, 0), (5, 0), (0, 0)))
 
-    xbc, sout = conv_and_state(meta, recv, halo, weight, ein, rows, e3, 0, seqs)
+    xbc = conv_slab(meta, recv, weight, 0, seqs)
+    xbc, sout = edge_and_state(meta, xbc, recv, halo, weight, ein, rows, e3, 0, seqs)
     sout, seed = lax.optimization_barrier((sout, seed))
     got = lax.all_to_all(sout, "z", 0, 0, tiled=True)
     part = inner_output(xbc, ein, eout, rows, e3, 0, seqs)

time: 208 us -> 211 us (1.014)
  Pallas kernels: 42.7 us -> 46.2 us
    pallas_call x1 -> x2, Pallas kernels: 10.4 us -> 13.8 us  [the longest x1 8.37 us: conv_slab(): pl.pallas_call(functools.partial(conv_body, first), grid_spec=pltpu.Prefe...]
  transfers between devices with their start and end apart: 14 -> 14, of which waited for: 9 -> 8; matrix products, arithmetic and copies ran while one was open for 4% -> 4% of each run, Pallas kernels for 13% -> 14%
where the time goes in v3:
time: 211 us; the launch traced here: 210 us
  waiting for transfers between devices  74.2 us (35%)
  Pallas kernels  46.2 us (22%)
  starting transfers between devices  43.2 us (20%)
  blocking collectives  36.4 us (17%)
  local copies, waits for them, and re-layouts  5.82 us (3%)
  other arithmetic  2.76 us (1%)
    all_to_all x1, blocking collectives, local(): got = lax.all_to_all(sout, 'z', 0, 0, tiled=True)  36.4 us
    all_to_all x1, waiting for transfers between devices, local(): token = lax.all_to_all(y, 'j', 0, 0, tiled=True)  31.5 us
    all_to_all x1, waiting for transfers between devices, local(): recv = lax.all_to_all(sent, 'j', 0, 0, tiled=True)  15.4 us
    all_to_all x1, waiting for transfers between devices, local(): back = lax.all_to_all(start, 'z', 0, 0, tiled=True)  13.4 us
    ppermute x6, starting transfers between devices, from_pools(): lax.ppermute(mine, 'pool', [(i, (i + k) % pools) for i in range(pools)])  8.49 us
    pallas_call x1, Pallas kernels, conv_slab(): pl.pallas_call(functools.partial(conv_body, first), grid_spec=pltpu.Prefe...  8.37 us
    pallas_call x1, Pallas kernels, inner_output(): pl.pallas_call(inner_body, grid=(count,), in_specs=[pl.BlockSpec((1, SLAB...  7.63 us
    all_to_all x1, starting transfers between devices, local(): token = lax.all_to_all(y, 'j', 0, 0, tiled=True)  7.55 us
  transfers between devices with their start and end apart: 14, of which 8 were waited for; matrix products, arithmetic and copies ran while one was open for 4% of the time, Pallas kernels for 14%

profile of v3, /device:TPU:1, one launch (start us, length us, event | category | flops | bytes accessed | tf_op | source)
XLA Modules:
  0.0 209.5 jit_solution(12010712509702221540)
XLA Ops:
  0.6 1.6 front_rows.1
  2.3 6.6 %all-to-all-start = ((bf16[8,208,128]{2,1,0:T(8,128)(2,1)}), bf16[8,208,128]{2,1,0:T(8,128)(2,1)S(1)}, u32[]{:S(2)}, u32[]{:S(2)}) async-start(bf16[8,208,128]{2,1,0:T(8,128)(2,1)} %front_rows.1), calls=%async_computation | async-start | bytes 851968 | tf_op jit(solution)/shard_map/all_to_all | solution.py:461
  8.9 3.9 %pack_groups.1 = bf16[8,3,64,1280]{3,2,1,0:T(8,128)(2,1)} custom-call(bf16[3,64,10240]{2,1,0:T(8,128)(2,1)} %x_ref.1), custom_call_target="tpu_custom_call" | custom-call | tf_op jit(solution)/shard_map/pack_groups/pallas_call | solution.py:86
  12.8 0.0 copy-start.4
  12.8 0.0 copy-start.5
  12.8 0.0 copy-start.6
  12.9 0.0 copy-start.7
  12.9 0.0 copy-start.2
  12.9 4.4 %all-to-all-done.dt_ref = bf16[8,208,128]{2,1,0:T(8,128)(2,1)S(1)} async-done(((bf16[8,208,128]{2,1,0:T(8,128)(2,1)}), bf16[8,208,128]{2,1,0:T(8,128)(2,1)S(1)}, u32[]{:S(2)}, u32[]{:S(2)}) %all-to-all-start) | async-done | bytes 426016 | tf_op jit(solution)/shard_map/all_to_all | solution.py:461
  17.3 5.3 %all-to-all-start.1 = ((bf16[8,3,64,1280]{3,2,1,0:T(8,128)(2,1)}), bf16[8,3,64,1280]{3,2,1,0:T(8,128)(2,1)}, u32[]{:S(2)}, u32[]{:S(2)}) async-start(bf16[8,3,64,1280]{3,2,1,0:T(8,128)(2,1)} %pack_groups.1), calls=%async_computation.1 | async-start | bytes 7864320 | tf_op jit(solution)/shard_map/all_to_all | solution.py:464
  22.6 0.7 constant_dynamic-slice_fusion.1
  23.3 0.8 constant_dynamic-slice_fusion.2
  24.2 0.0 copy-done.4
  24.2 0.0 copy-done.5
  24.2 0.1 compare_and_fusion
  24.3 0.7 constant_dynamic-slice_fusion.4
  25.0 0.7 constant_dynamic-slice_fusion.5
  25.8 2.9 %collective-permute-start = (bf16[8,16,128]{2,1,0:T(8,128)(2,1)S(1)}, bf16[8,16,128]{2,1,0:T(8,128)(2,1)S(1)}, u32[]{:S(2)}, u32[]{:S(2)}) collective-permute-start(bf16[8,16,128]{2,1,0:T(8,128)(2,1)S(1)} %slice.6), channel_id=1, source_target_pairs={{0,0},{4,32},{8,64},{12,96},{16,128},{20,160},{24,192},{28,224},{3... | collective-permute-start | bytes 98312 | tf_op jit(solution)/shard_map/ppermute | solution.py:480
  28.8 0.0 copy-done.6
  28.8 0.1 dynamic-slice_convert_fusion
  28.9 0.1 dynamic_slice.30
  28.9 2.5 %collective-permute-done.par_ref = bf16[8,16,128]{2,1,0:T(8,128)(2,1)S(1)} collective-permute-done((bf16[8,16,128]{2,1,0:T(8,128)(2,1)S(1)}, bf16[8,16,128]{2,1,0:T(8,128)(2,1)S(1)}, u32[]{:S(2)}, u32[]{:S(2)}) %collective-permute-start) | collective-permute-done | bytes 32800 | tf_op jit(solution)/shard_map/ppermute | solution.py:480
  31.5 0.6 collective-permute-start.1
  32.0 2.5 %collective-permute-start.2 = (bf16[8,128,128]{2,1,0:T(8,128)(2,1)S(1)}, bf16[8,128,128]{2,1,0:T(8,128)(2,1)S(1)}, u32[]{:S(2)}, u32[]{:S(2)}) collective-permute-start(bf16[8,128,128]{2,1,0:T(8,128)(2,1)S(1)} %bitcast.11), channel_id=1, source_target_pairs={{0,2},{1,3},{2,0},{3,1},{4,6},{5,7},{6,4},{7,5},{8,10},{9,11},{10,... | collective-permute-start | bytes 786440 | tf_op jit(solution)/shard_map/ppermute | solution.py:477
  34.5 1.2 collective-permute-start.3
  35.6 0.1 pad_add_fusion.meta_ref
  35.7 0.1 and_convert_fusion.e3_ref
  35.9 4.1 %step_factors.1 = (bf16[3,512,128]{2,1,0:T(8,128)(2,1)S(1)}, bf16[3,512,128]{2,1,0:T(8,128)(2,1)S(1)}, bf16[3,16,128]{2,1,0:T(8,128)(2,1)S(1)}) custom-call(s32[5]{0:T(128)S(1)} %pad_add_fusion.meta_ref, bf16[8,208,128]{2,1,0:T(8,128)(2,1)S(1)} %all-to-all-done.dt_ref, bf16[8,16,128]{2,1,0:T(8,128)(2,1)S(1)} %collective-permute-done.par_ref), custom_call_target="tpu_custom_call" | custom-call | tf_op jit(solution)/shard_map/step_factors/pallas_call | solution.py:157
  40.0 0.0 collective-permute-done.1
  40.0 2.5 %collective-permute-done.2 = bf16[8,128,128]{2,1,0:T(8,128)(2,1)S(1)} collective-permute-done((bf16[8,128,128]{2,1,0:T(8,128)(2,1)S(1)}, bf16[8,128,128]{2,1,0:T(8,128)(2,1)S(1)}, u32[]{:S(2)}, u32[]{:S(2)}) %collective-permute-start.2) | collective-permute-done | bytes 262176 | tf_op jit(solution)/shard_map/ppermute | solution.py:477
  42.5 0.7 copy-done.3
  43.2 0.2 collective-permute-done.3
  43.4 1.2 pad_maximum_fusion
  44.6 0.6 gather_fusion
  45.2 0.1 select_multiply_fusion
  45.3 1.6 collective-permute-start.4
  46.8 2.1 collective-permute-start.5
  48.9 0.7 collective-permute-start.6
  49.6 3.8 %collective-permute-start.8 = (bf16[3,128,128]{2,1,0:T(8,128)(2,1)S(1)}, bf16[3,128,128]{2,1,0:T(8,128)(2,1)S(1)}, u32[]{:S(2)}, u32[]{:S(2)}) collective-permute-start(bf16[3,128,128]{2,1,0:T(8,128)(2,1)S(1)} %select_multiply_fusion), channel_id=1, source_target_pairs={{0,0},{4,32},{8,64},{12,96},{16,128},{20,160},{24,192},{28,224},{3... | collective-permute-start | bytes 294920 | tf_op jit(solution)/shard_map/ppermute | solution.py:486
  53.4 15.4 %all-to-all-done.1.recv_ref.raw_ref = bf16[8,3,64,1280]{3,2,1,0:T(8,128)(2,1)} async-done(((bf16[8,3,64,1280]{3,2,1,0:T(8,128)(2,1)}), bf16[8,3,64,1280]{3,2,1,0:T(8,128)(2,1)}, u32[]{:S(2)}, u32[]{:S(2)}) %all-to-all-start.1) | async-done | bytes 3932192 | tf_op jit(solution)/shard_map/all_to_all | solution.py:464
  68.8 0.8 slice_bitcast_fusion
  69.7 2.9 %collective-permute-start.7 = (bf16[3,3,1280]{2,1,0:T(4,128)(2,1)S(1)}, bf16[3,3,1280]{2,1,0:T(4,128)(2,1)S(1)}, u32[]{:S(2)}, u32[]{:S(2)}) collective-permute-start(bf16[3,3,1280]{2,1,0:T(4,128)(2,1)S(1)} %slice_bitcast_fusion), channel_id=1, source_target_pairs={{0,32},{32,64},{64,96},{96,128},{128,160},{160,192},{192,224},{1,3... | collective-permute-start | bytes 69128 | tf_op jit(solution)/shard_map/ppermute | solution.py:494
  72.6 0.0 collective-permute-done.4
  72.6 0.0 collective-permute-done.5
  72.6 0.0 collective-permute-done.6
  72.6 0.2 pad_maximum_fusion.1
  72.8 0.6 gather_fusion.1
  73.4 8.4 %conv_slab.1.xbc_ref = bf16[3,512,1280]{2,1,0:T(8,128)(2,1)} custom-call(s32[5]{0:T(128)S(1)} %pad_add_fusion.meta_ref, bf16[8,3,64,1280]{3,2,1,0:T(8,128)(2,1)} %all-to-all-done.1.recv_ref.raw_ref, f32[4,1280]{1,0:T(4,128)S(1)} %maximum_multiply_fusion.w_ref), custom_call_target="tpu_custom_call" | custom-call | tf_op jit(solution)/shard_map/conv_slab/pallas_call | solution.py:209
  81.8 0.0 collective-permute-done.7
  81.8 0.1 multiply_select_fusion
  81.9 5.5 %edge_and_state.1 = (bf16[3,512,1280]{2,1,0:T(8,128)(2,1)}, bf16[8,3,144,128]{3,2,1,0:T(8,128)(2,1)}) custom-call(s32[5]{0:T(128)S(1)} %pad_add_fusion.meta_ref, bf16[3,512,1280]{2,1,0:T(8,128)(2,1)} %conv_slab.1.xbc_ref, bf16[8,3,64,1280]{3,2,1,0:T(8,128)(2,1)} %all-to-all-done.1.recv_ref.raw_ref, ...), custom_call_target="tpu_custom_call", output_to_operand_aliasing={{0}: (1, {})} | custom-call | tf_op jit(solution)/shard_map/edge_and_state/pallas_call | solution.py:256
  87.4 0.0 collective-permute-done.8.seed_ref
  87.4 36.4 %all_to_all.25.got_ref = bf16[8,3,144,128]{3,2,1,0:T(8,128)(2,1)S(1)} all-to-all(bf16[8,3,144,128]{3,2,1,0:T(8,128)(2,1)} %get-tuple-element.30), channel_id=1, replica_groups=mesh['z'=8,'j'=8,'pool'=4] {'z'}, dimensions={0} | all-to-all | bytes 1769472 | tf_op jit(solution)/shard_map/all_to_all | solution.py:501
  123.8 1.9 scan_slabs.1
  125.7 3.5 %all-to-all-start.3 = ((bf16[8,3,128,128]{3,2,1,0:T(8,128)(2,1)}), bf16[8,3,128,128]{3,2,1,0:T(8,128)(2,1)S(1)}, u32[]{:S(2)}, u32[]{:S(2)}) async-start(bf16[8,3,128,128]{3,2,1,0:T(8,128)(2,1)} %get-tuple-element.32), calls=%async_computation.3 | async-start | bytes 1572864 | tf_op jit(solution)/shard_map/all_to_all | solution.py:504
  129.2 7.6 %inner_output.1.part_ref = f32[3,512,1024]{2,1,0:T(8,128)} custom-call(bf16[3,512,1280]{2,1,0:T(8,128)(2,1)} %get-tuple-element.26.xbc_ref.c_ref, bf16[3,512,128]{2,1,0:T(8,128)(2,1)S(1)} %get-tuple-element.24.ein_ref, bf16[3,512,128]{2,1,0:T(8,128)(2,1)S(1)} %get-tuple-element.27.eout_ref, bf16[3,16,128]{2,1,0:T(8,128)(2,1)S(1)} %get-tuple-element.25.rows_ref, ...), custom_call_target="tpu_custom_call" | custom-call | tf_op jit(solution)/shard_map/inner_output/pallas_call | solution.py:306
  136.9 13.4 %all-to-all-done.3.start_ref = bf16[8,3,128,128]{3,2,1,0:T(8,128)(2,1)S(1)} async-done(((bf16[8,3,128,128]{3,2,1,0:T(8,128)(2,1)}), bf16[8,3,128,128]{3,2,1,0:T(8,128)(2,1)S(1)}, u32[]{:S(2)}, u32[]{:S(2)}) %all-to-all-start.3) | async-done | bytes 786464 | tf_op jit(solution)/shard_map/all_to_all | solution.py:504
  150.3 7.1 %finish_output.1 = bf16[8,3,64,1024]{3,2,1,0:T(8,128)(2,1)} custom-call(f32[3,512,1024]{2,1,0:T(8,128)} %inner_output.1.part_ref, bf16[3,512,1280]{2,1,0:T(8,128)(2,1)} %get-tuple-element.26.xbc_ref.c_ref, bf16[8,3,128,128]{3,2,1,0:T(8,128)(2,1)S(1)} %all-to-all-done.3.start_ref, bf16[3,512,128]{2,1,0:T(8,128)(2,1)S(1)} %get-tuple-element.27.eout_ref, ...), custom_call_target="tpu_custom_call" | custom-call | tf_op jit(solution)/shard_map/finish_output/pallas_call | solution.py:368
  157.4 7.6 %all-to-all-start.4 = ((bf16[8,3,64,1024]{3,2,1,0:T(8,128)(2,1)}), bf16[8,3,64,1024]{3,2,1,0:T(8,128)(2,1)}, u32[]{:S(2)}, u32[]{:S(2)}) async-start(bf16[8,3,64,1024]{3,2,1,0:T(8,128)(2,1)} %finish_output.1), calls=%async_computation.4 | async-start | bytes 6291456 | tf_op jit(solution)/shard_map/all_to_all | solution.py:507
  164.9 2.2 %collective-permute-start.9 = (bf16[3,128,128]{2,1,0:T(8,128)(2,1)S(1)}, bf16[3,128,128]{2,1,0:T(8,128)(2,1)S(1)}, u32[]{:S(2)}, u32[]{:S(2)}) collective-permute-start(bf16[3,128,128]{2,1,0:T(8,128)(2,1)S(1)} %get-tuple-element.33), channel_id=1, source_target_pairs={{0,0},{4,32},{8,64},{12,96},{16,128},{20,160},{24,192},{28,224},{3... | collective-permute-start | bytes 294920 | tf_op jit(solution)/shard_map/ppermute | solution.py:505
  167.1 4.1 %collective-permute-done.9 = bf16[3,128,128]{2,1,0:T(8,128)(2,1)S(1)} collective-permute-done((bf16[3,128,128]{2,1,0:T(8,128)(2,1)S(1)}, bf16[3,128,128]{2,1,0:T(8,128)(2,1)S(1)}, u32[]{:S(2)}, u32[]{:S(2)}) %collective-permute-start.9) | collective-permute-done | bytes 98336 | tf_op jit(solution)/shard_map/ppermute | solution.py:505
  171.2 0.7 convert.3
  171.9 31.5 %all-to-all-done.4.y_ref = bf16[8,3,64,1024]{3,2,1,0:T(8,128)(2,1)} async-done(((bf16[8,3,64,1024]{3,2,1,0:T(8,128)(2,1)}), bf16[8,3,64,1024]{3,2,1,0:T(8,128)(2,1)}, u32[]{:S(2)}, u32[]{:S(2)}) %all-to-all-start.4) | async-done | bytes 3145760 | tf_op jit(solution)/shard_map/all_to_all | solution.py:507
  203.4 6.1 %gated_norm.1 = bf16[3,64,8192]{2,1,0:T(8,128)(2,1)} custom-call(s32[5]{0:T(128)S(1)} %pad_add_fusion.meta_ref, bf16[8,3,64,1024]{3,2,1,0:T(8,128)(2,1)} %all-to-all-done.4.y_ref, bf16[3,64,8192]{2,1,0:T(8,128)(2,1)S(1)} %copy-done, f32[1,8192]{1,0:T(1,128)S(1)} %bitcast.9), custom_call_target="tpu_custom_call" | custom-call | tf_op jit(solution)/shard_map/gated_norm/pallas_call | solution.py:407
  (18 shorter events, 0.2 us)
Async XLA Ops:
  2.3 15.1 %all-to-all-start = ((bf16[8,208,128]{2,1,0:T(8,128)(2,1)}), bf16[8,208,128]{2,1,0:T(8,128)(2,1)S(1)}, u32[]{:S(2)}, u32[]{:S(2)}) async-start(bf16[8,208,128]{2,1,0:T(8,128)(2,1)} %front_rows.1), calls=%async_computation | async-start | bytes 851968 | tf_op jit(solution)/shard_map/all_to_all | solution.py:461
  12.8 11.4 %copy-start.4 = (s32[12]{0:T(128)S(1)}, s32[12]{0:T(128)}, u32[]{:S(2)}) copy-start(s32[12]{0:T(128)} %param.25) | copy-start | bytes 148
  12.8 11.4 %copy-start.5 = (s32[12]{0:T(128)S(1)}, s32[12]{0:T(128)}, u32[]{:S(2)}) copy-start(s32[12]{0:T(128)} %param.24) | copy-start | bytes 148
  12.8 15.9 %copy-start.6 = (s32[12]{0:T(128)S(1)}, s32[12]{0:T(128)}, u32[]{:S(2)}) copy-start(s32[12]{0:T(128)} %param.26) | copy-start | bytes 148
  12.9 16.0 %copy-start.7 = (s32[12]{0:T(128)S(1)}, s32[12]{0:T(128)}, u32[]{:S(2)}) copy-start(s32[12]{0:T(128)} %param.27) | copy-start | bytes 148
  12.9 18.6 %copy-start.2 = (bf16[8,2,64,128]{3,2,1,0:T(8,128)(2,1)S(1)}, bf16[8,2,64,128]{3,2,1,0:T(8,128)(2,1)}, u32[]{:S(2)}) copy-start(bf16[8,2,64,128]{3,2,1,0:T(8,128)(2,1)} %param.22) | copy-start | bytes 786436
  17.3 51.5 %all-to-all-start.1 = ((bf16[8,3,64,1280]{3,2,1,0:T(8,128)(2,1)}), bf16[8,3,64,1280]{3,2,1,0:T(8,128)(2,1)}, u32[]{:S(2)}, u32[]{:S(2)}) async-start(bf16[8,3,64,1280]{3,2,1,0:T(8,128)(2,1)} %pack_groups.1), calls=%async_computation.1 | async-start | bytes 7864320 | tf_op jit(solution)/shard_map/all_to_all | solution.py:464
  25.8 5.6 %collective-permute-start = (bf16[8,16,128]{2,1,0:T(8,128)(2,1)S(1)}, bf16[8,16,128]{2,1,0:T(8,128)(2,1)S(1)}, u32[]{:S(2)}, u32[]{:S(2)}) collective-permute-start(bf16[8,16,128]{2,1,0:T(8,128)(2,1)S(1)} %slice.6), channel_id=1, source_target_pairs={{0,0},{4,32},{8,64},{12,96},{16,128},{20,160},{24,192},{28,224},{3... | collective-permute-start | bytes 98312 | tf_op jit(solution)/shard_map/ppermute | solution.py:480
  31.5 8.5 %collective-permute-start.1 = (bf16[8,128,128]{2,1,0:T(8,128)(2,1)S(1)}, bf16[8,128,128]{2,1,0:T(8,128)(2,1)S(1)}, u32[]{:S(2)}, u32[]{:S(2)}) collective-permute-start(bf16[8,128,128]{2,1,0:T(8,128)(2,1)S(1)} %bitcast.10), channel_id=1, source_target_pairs={{0,1},{1,2},{2,3},{3,0},{4,5},{5,6},{6,7},{7,4},{8,9},{9,10},{10,1... | collective-permute-start | bytes 786440 | tf_op jit(solution)/shard_map/ppermute | solution.py:477
  32.0 10.5 %collective-permute-start.2 = (bf16[8,128,128]{2,1,0:T(8,128)(2,1)S(1)}, bf16[8,128,128]{2,1,0:T(8,128)(2,1)S(1)}, u32[]{:S(2)}, u32[]{:S(2)}) collective-permute-start(bf16[8,128,128]{2,1,0:T(8,128)(2,1)S(1)} %bitcast.11), channel_id=1, source_target_pairs={{0,2},{1,3},{2,0},{3,1},{4,6},{5,7},{6,4},{7,5},{8,10},{9,11},{10,... | collective-permute-start | bytes 786440 | tf_op jit(solution)/shard_map/ppermute | solution.py:477
  34.5 9.0 %collective-permute-start.3 = (bf16[8,128,128]{2,1,0:T(8,128)(2,1)S(1)}, bf16[8,128,128]{2,1,0:T(8,128)(2,1)}, u32[]{:S(2)}, u32[]{:S(2)}) collective-permute-start(bf16[8,128,128]{2,1,0:T(8,128)(2,1)S(1)} %bitcast.12), channel_id=1, source_target_pairs={{0,3},{1,0},{2,1},{3,2},{4,7},{5,4},{6,5},{7,6},{8,11},{9,8},{10,9... | collective-permute-start | bytes 786440 | tf_op jit(solution)/shard_map/ppermute | solution.py:477
  42.5 0.7 copy-start.3
  45.3 27.3 %collective-permute-start.4 = (bf16[8,3,1280]{2,1,0:T(4,128)(2,1)S(1)}, bf16[8,3,1280]{2,1,0:T(4,128)(2,1)S(1)}, u32[]{:S(2)}, u32[]{:S(2)}) collective-permute-start(bf16[8,3,1280]{2,1,0:T(4,128)(2,1)S(1)} %pad_maximum_fusion.2), channel_id=1, source_target_pairs={{0,1},{1,2},{2,3},{3,0},{4,5},{5,6},{6,7},{7,4},{8,9},{9,10},{10,1... | collective-permute-start | bytes 184328 | tf_op jit(solution)/shard_map/ppermute | solution.py:477
  46.8 25.7 %collective-permute-start.5 = (bf16[8,3,1280]{2,1,0:T(4,128)(2,1)S(1)}, bf16[8,3,1280]{2,1,0:T(4,128)(2,1)S(1)}, u32[]{:S(2)}, u32[]{:S(2)}) collective-permute-start(bf16[8,3,1280]{2,1,0:T(4,128)(2,1)S(1)} %pad_maximum_fusion.2), channel_id=1, source_target_pairs={{0,2},{1,3},{2,0},{3,1},{4,6},{5,7},{6,4},{7,5},{8,10},{9,11},{10,... | collective-permute-start | bytes 184328 | tf_op jit(solution)/shard_map/ppermute | solution.py:477
  48.9 23.7 %collective-permute-start.6 = (bf16[8,3,1280]{2,1,0:T(4,128)(2,1)S(1)}, bf16[8,3,1280]{2,1,0:T(4,128)(2,1)S(1)}, u32[]{:S(2)}, u32[]{:S(2)}) collective-permute-start(bf16[8,3,1280]{2,1,0:T(4,128)(2,1)S(1)} %pad_maximum_fusion.2), channel_id=1, source_target_pairs={{0,3},{1,0},{2,1},{3,2},{4,7},{5,4},{6,5},{7,6},{8,11},{9,8},{10,9... | collective-permute-start | bytes 184328 | tf_op jit(solution)/shard_map/ppermute | solution.py:477
  49.6 37.8 %collective-permute-start.8 = (bf16[3,128,128]{2,1,0:T(8,128)(2,1)S(1)}, bf16[3,128,128]{2,1,0:T(8,128)(2,1)S(1)}, u32[]{:S(2)}, u32[]{:S(2)}) collective-permute-start(bf16[3,128,128]{2,1,0:T(8,128)(2,1)S(1)} %select_multiply_fusion), channel_id=1, source_target_pairs={{0,0},{4,32},{8,64},{12,96},{16,128},{20,160},{24,192},{28,224},{3... | collective-permute-start | bytes 294920 | tf_op jit(solution)/shard_map/ppermute | solution.py:486
  69.7 12.1 %collective-permute-start.7 = (bf16[3,3,1280]{2,1,0:T(4,128)(2,1)S(1)}, bf16[3,3,1280]{2,1,0:T(4,128)(2,1)S(1)}, u32[]{:S(2)}, u32[]{:S(2)}) collective-permute-start(bf16[3,3,1280]{2,1,0:T(4,128)(2,1)S(1)} %slice_bitcast_fusion), channel_id=1, source_target_pairs={{0,32},{32,64},{64,96},{96,128},{128,160},{160,192},{192,224},{1,3... | collective-permute-start | bytes 69128 | tf_op jit(solution)/shard_map/ppermute | solution.py:494
  125.7 24.6 %all-to-all-start.3 = ((bf16[8,3,128,128]{3,2,1,0:T(8,128)(2,1)}), bf16[8,3,128,128]{3,2,1,0:T(8,128)(2,1)S(1)}, u32[]{:S(2)}, u32[]{:S(2)}) async-start(bf16[8,3,128,128]{3,2,1,0:T(8,128)(2,1)} %get-tuple-element.32), calls=%async_computation.3 | async-start | bytes 1572864 | tf_op jit(solution)/shard_map/all_to_all | solution.py:504
  157.3 46.0 %copy-start = (bf16[3,64,8192]{2,1,0:T(8,128)(2,1)S(1)}, bf16[3,64,8192]{2,1,0:T(8,128)(2,1)}, u32[]{:S(2)}) copy-start(bf16[3,64,8192]{2,1,0:T(8,128)(2,1)} %gate_ref.1) | copy-start | bytes 9437188
  157.4 46.1 %copy-start.1 = (f32[8192]{0:T(1024)S(1)}, f32[8192]{0:T(1024)}, u32[]{:S(2)}) copy-start(f32[8192]{0:T(1024)} %param.21) | copy-start | bytes 98308
  157.4 46.0 %all-to-all-start.4 = ((bf16[8,3,64,1024]{3,2,1,0:T(8,128)(2,1)}), bf16[8,3,64,1024]{3,2,1,0:T(8,128)(2,1)}, u32[]{:S(2)}, u32[]{:S(2)}) async-start(bf16[8,3,64,1024]{3,2,1,0:T(8,128)(2,1)} %finish_output.1), calls=%async_computation.4 | async-start | bytes 6291456 | tf_op jit(solution)/shard_map/all_to_all | solution.py:507
  164.9 6.3 %collective-permute-start.9 = (bf16[3,128,128]{2,1,0:T(8,128)(2,1)S(1)}, bf16[3,128,128]{2,1,0:T(8,128)(2,1)S(1)}, u32[]{:S(2)}, u32[]{:S(2)}) collective-permute-start(bf16[3,128,128]{2,1,0:T(8,128)(2,1)S(1)} %get-tuple-element.33), channel_id=1, source_target_pairs={{0,0},{4,32},{8,64},{12,96},{16,128},{20,160},{24,192},{28,224},{3... | collective-permute-start | bytes 294920 | tf_op jit(solution)/shard_map/ppermute | solution.py:505
